TPU v7x, 32 devices: a whole 2x2x4 slice. The times are simulated.
32 devices in a mesh: dp: 8 (over z, x), mp: 4 (over y, core).
Axes of the slice: x: 2, y: 2, z: 4, core: 2. Of those that a mesh axis runs over, the one named last changes fastest.
Arguments:
- tokens: bfloat16 [16384, 768], P(('dp', 'mp')), may hold values from -6 to 6
- lengths: int32 [8, 16], P('dp'), may hold values from 1 to 1024, 2048 in all within a row
- w_qkv: bfloat16 [768, 3, 768], P(None, None, 'mp'), may hold values from -0.21875 to 0.21875
- w_out: bfloat16 [768, 768], P('mp'), may hold values from -0.875 to 0.875
- w_gate_up: bfloat16 [768, 2, 3072], P(None, None, 'mp'), may hold values from -0.21875 to 0.21875
- w_down: bfloat16 [3072, 768], P('mp'), may hold values from -0.109375 to 0.109375
- ln1_scale: float32 [768], replicated, may hold values from 0.5 to 1.5
- ln1_shift: float32 [768], replicated, may hold values from -2 to 2
- ln2_scale: float32 [768], replicated, may hold values from 0.5 to 1.5
- ln2_shift: float32 [768], replicated, may hold values from -2 to 2
- cotangent: bfloat16 [16384, 768], P(('dp', 'mp')), may hold values from -6 to 6
Outputs:
- output: bfloat16 [16384, 768], P(('dp', 'mp'))
- d_tokens: bfloat16 [16384, 768], P(('dp', 'mp'))
- grad_w_qkv: float32 [768, 3, 768], P(None, None, 'mp')
- grad_w_out: float32 [768, 768], P('mp')
- grad_w_gate_up: float32 [768, 2, 3072], P(None, None, 'mp')
- grad_w_down: float32 [3072, 768], P('mp')
- grad_ln1_scale: float32 [768], P('mp')
- grad_ln1_shift: float32 [768], P('mp')
- grad_ln2_scale: float32 [768], P('mp')
- grad_ln2_shift: float32 [768], P('mp')
Inputs may be any that keep to these rules, and one draw needn't show every extreme that they name: The 16 lengths of each row sum to 2048, and each row's longest is exactly 1024.
All inputs are finite; a program needn't handle non-finite values.
Results may differ from a plain program's by a relative error of at most 0.024.
Values may be sent and summed in bfloat16 or wider, within the bound.
A program may use at most 192 MiB of HBM per device.

v0:
```python
import functools
import math

import jax
import jax.numpy as jnp
from jax import lax
from jax.experimental import pallas as pl
from jax.experimental.pallas import tpu as pltpu
from jax.sharding import PartitionSpec as P

F32 = jnp.float32
BF16 = jnp.bfloat16
HEAD_DIM = 64
LANES = 128
EPSILON = 1e-05
KEYS = 512
FAR = -(2.0**100)
LOG2E = math.log2(math.e)
NT = (((1,), (1,)), ((), ()))
TN = (((0,), (0,)), ((), ()))
NN = (((1,), (0,)), ((), ()))
VMEM_LIMIT = 58 << 20
WIDE_LIMIT = 62 << 20
MESH = pl.DeviceIdType.MESH


def mm(a, b, dims=NN):
    return lax.dot_general(a, b, dims, preferred_element_type=F32)


def thirds(row):
    high = row.astype(BF16).astype(F32)
    mid = (row - high).astype(BF16).astype(F32)
    low = row - high - mid
    return jnp.concatenate([high, mid, low, jnp.zeros((13, row.shape[1]), F32)], axis=0)


def slot_of(relative):
    return relative // 2 + 2 * (relative % 2)


def span(index, size):
    return pl.ds(pl.multiple_of(index * size, size), size)


def project_kernel(place, x_ref, w_ref, cos_ref, sin_ref, bounds_ref, q_ref, k_ref, v_ref, k_rows_ref):
    rows = x_ref.shape[1]
    heads = q_ref.shape[0]
    width = heads * HEAD_DIM
    shard = place[0] ^ place[1 + pl.program_id(0)]
    projected = mm(w_ref[...], x_ref[0], NT)
    cosine, sine = cos_ref[...], sin_ref[...]
    token = lax.broadcasted_iota(jnp.int32, (16, rows), 1) + shard * rows
    inside = (token >= bounds_ref[:, 0:1]) & (token < bounds_ref[:, 1:2])
    row = lax.broadcasted_iota(jnp.int32, (48, rows), 0)
    q_tail = jnp.concatenate([jnp.where(inside, 0.0, FAR), jnp.zeros((48 - 16 + 16, rows), F32)], axis=0)
    ones = jnp.where(row < 3, 1.0, 0.0)
    k_tail = jnp.concatenate([jnp.where(inside, 1.0, 0.0), ones], axis=0)
    v_tail = jnp.concatenate([ones, jnp.zeros((16, rows), F32)], axis=0)
    half = HEAD_DIM // 2

    def rotated(start):
        first, second = projected[start : start + half], projected[start + half : start + HEAD_DIM]
        return first * cosine - second * sine, second * cosine + first * sine

    scale = LOG2E / math.sqrt(HEAD_DIM)
    for h in range(heads):
        first, second = rotated(h * HEAD_DIM)
        q_ref[h] = jnp.concatenate([first * scale, second * scale, q_tail], axis=0).astype(BF16)
        first, second = rotated(width + h * HEAD_DIM)
        k = jnp.concatenate([first, second, k_tail], axis=0)
        k_ref[h] = k.astype(BF16)
        k_rows_ref[h] = k.T.astype(BF16)
        start = 2 * width + h * HEAD_DIM
        v_ref[h] = jnp.concatenate([projected[start : start + HEAD_DIM], v_tail], axis=0).astype(BF16)


def project(x_slots, w_turned, cosine, sine, bounds, place, heads):
    count, rows, width = x_slots.shape
    tokens = count * rows
    along = jax.ShapeDtypeStruct((heads, LANES, tokens), BF16)
    down = jax.ShapeDtypeStruct((heads, tokens, LANES), BF16)
    whole = lambda *shape: pl.BlockSpec(shape, lambda s, place: (0,) * len(shape))
    table = pl.BlockSpec((HEAD_DIM // 2, rows), lambda s, place: (0, place[0] ^ place[1 + s]))
    along_spec = pl.BlockSpec((heads, LANES, rows), lambda s, place: (0, 0, place[0] ^ place[1 + s]))
    down_spec = pl.BlockSpec((heads, rows, LANES), lambda s, place: (0, place[0] ^ place[1 + s], 0))
    return pl.pallas_call(
        project_kernel,
        out_shape=(along, along, along, down),
        grid_spec=pltpu.PrefetchScalarGridSpec(
            num_scalar_prefetch=1,
            grid=(count,),
            in_specs=[
                pl.BlockSpec((1, rows, width), lambda s, place: (s, 0, 0)),
                whole(*w_turned.shape),
                table,
                table,
                whole(*bounds.shape),
            ],
            out_specs=[along_spec] * 3 + [down_spec],
        ),
        compiler_params=pltpu.CompilerParams(vmem_limit_bytes=VMEM_LIMIT),
        cost_estimate=pl.CostEstimate(
            flops=2 * tokens * width * w_turned.shape[0],
            bytes_accessed=tokens * width * 2 + 4 * heads * tokens * LANES * 2,
            transcendentals=0,
        ),
        name="project",
    )(place, x_slots, w_turned, cosine, sine, bounds)


def attend_kernel(place, ranges, q_ref, k_ref, v_ref, o_ref, o_along_ref, q_rows_ref, top_ref, acc_ref):
    heads = q_ref.shape[0]
    i = pl.program_id(0)
    tiles = pl.num_programs(0)
    top_ref[...] = jnp.full_like(top_ref, FAR)
    acc_ref[...] = jnp.zeros_like(acc_ref)

    def over_keys(j, carry):
        for h in range(heads):
            s = mm(k_ref[h, span(j, KEYS), :], q_ref[h])
            old = top_ref[h, 0:1, :]
            top = jnp.maximum(old, jnp.max(s, axis=0, keepdims=True))
            probs = jnp.exp2(s - top).astype(BF16)
            top_ref[h, 0:1, :] = top
            acc_ref[h] = acc_ref[h] * jnp.exp2(old - top) + mm(v_ref[h, :80, span(j, KEYS)], probs)
        return carry

    lax.fori_loop(ranges[i], ranges[tiles + i] + 1, over_keys, 0)
    outs = []
    for h in range(heads):
        total = acc_ref[h, HEAD_DIM : HEAD_DIM + 1, :]
        outs.append(acc_ref[h, :HEAD_DIM, :] / total)
        level = top_ref[h, 0:1, :] + jnp.log2(total)
        query = q_ref[h].astype(F32)
        q_rows_ref[h] = jnp.concatenate([query[:80], thirds(-level), query[96:]], axis=0).T.astype(BF16)
    out = jnp.concatenate(outs, axis=0)
    o_along_ref[...] = out.astype(BF16)
    o_ref[0] = out.T.astype(BF16)


def attend(q, k_rows, v, place, ranges, shards):
    heads, _, tokens = q.shape
    rows = tokens // shards
    whole = lambda *shape: pl.BlockSpec(shape, lambda i, place, ranges: (0, 0, 0))
    return pl.pallas_call(
        attend_kernel,
        out_shape=(
            jax.ShapeDtypeStruct((shards, rows, heads * HEAD_DIM), BF16),
            jax.ShapeDtypeStruct((heads * HEAD_DIM, tokens), BF16),
            jax.ShapeDtypeStruct((heads, tokens, LANES), BF16),
        ),
        grid_spec=pltpu.PrefetchScalarGridSpec(
            num_scalar_prefetch=2,
            grid=(shards,),
            in_specs=[
                pl.BlockSpec((heads, LANES, rows), lambda i, place, ranges: (0, 0, i)),
                whole(heads, tokens, LANES),
                whole(heads, LANES, tokens),
            ],
            out_specs=[
                pl.BlockSpec(
                    (1, rows, heads * HEAD_DIM), lambda i, place, ranges: (slot_of(i ^ place[0]), 0, 0)
                ),
                pl.BlockSpec((heads * HEAD_DIM, rows), lambda i, place, ranges: (0, i)),
                pl.BlockSpec((heads, rows, LANES), lambda i, place, ranges: (0, i, 0)),
            ],
            scratch_shapes=[pltpu.VMEM((heads, 8, rows), F32), pltpu.VMEM((heads, 80, rows), F32)],
        ),
        compiler_params=pltpu.CompilerParams(vmem_limit_bytes=VMEM_LIMIT),
        cost_estimate=pl.CostEstimate(
            flops=2 * heads * tokens * tokens * LANES,
            bytes_accessed=5 * heads * tokens * LANES * 2,
            transcendentals=heads * tokens * tokens // 2,
        ),
        name="attend",
    )(place, ranges, q, k_rows, v)


def doc_tables(lengths, tokens, rows):
    ends = jnp.cumsum(lengths)
    starts = ends - lengths
    places = jnp.arange(tokens, dtype=jnp.int32)
    inside = (places[:, None] >= starts[None, :]) & (places[:, None] < ends[None, :])
    positions = places - jnp.sum(jnp.where(inside, starts[None, :], 0), axis=1)

    def shared(size, other):
        edge = jnp.arange(tokens // size, dtype=jnp.int32) * size
        touches = (starts[None, :] < edge[:, None] + size) & (ends[None, :] > edge[:, None])
        first = jnp.min(jnp.where(touches, starts[None, :], tokens), axis=1) // other
        last = (jnp.max(jnp.where(touches, ends[None, :], 0), axis=1) - 1) // other
        return jnp.concatenate([first, last]).astype(jnp.int32)

    bounds = jnp.stack([starts, ends], axis=1).astype(jnp.int32)
    return positions, shared(rows, KEYS), bounds


def rotary(positions):
    rate = jnp.exp(jnp.arange(HEAD_DIM // 2, dtype=F32) * (-2.0 * math.log(1000.0) / HEAD_DIM))
    angles = rate[:, None] * positions.astype(F32)[None, :]
    return jnp.cos(angles), jnp.sin(angles)


def dp_orders(size):
    bits = list(range(size.bit_length() - 1))
    return [bits, bits[1::-1] + bits[2:]]


def halvings(size):
    return min(3, size.bit_length() - 1)


def peer_of(index, bit):
    mine = (index // (1 << bit)) % 2
    return index + (1 - 2 * mine) * (1 << bit), mine


def send(source, target, send_sem, recv_sem, partner):
    copy = pltpu.make_async_remote_copy(
        source, target, send_sem, recv_sem, device_id=partner, device_id_type=MESH
    )
    copy.start()
    return copy


def greet(partners):
    barrier = pltpu.get_barrier_semaphore()
    for partner in partners:
        pl.semaphore_signal(barrier, inc=1, device_id=partner, device_id_type=MESH)
    pl.semaphore_wait(barrier, len(partners))


ATT, BRANCH, NORMED, OUT, DOUT, DNORMED, DH, DH_NEAR, DH_LAST, GRAD_NEAR, GRAD_DP = range(11)


def middle_kernel(
    size, att_ref, wo_ref, wo_near_ref, tok_ref, cot_ref, ln_ref, win_hbm, win_near_hbm, wdn_hbm, wdn_near_hbm,
    out_ref, dh_ref, slots_ref, norms_ref, kept_hbm,
    win, wdn, near, outbox, inbox, low, hat, res, own, r1, gu, hid, dlow, total, give, take, take_dp, sums,
    sems, loads, stores,
):
    rows, width = tok_ref.shape
    hidden = wdn.shape[0] // 2
    half = width // 2
    chunk = rows // 2
    chunks = [slice(c * chunk, (c + 1) * chunk) for c in range(2)]
    m, me = lax.axis_index("mp"), lax.axis_index("dp")
    core, far = {"mp": peer_of(m, 0)[0]}, {"mp": peer_of(m, 1)[0]}
    firsts = [order[0] for order in dp_orders(size)]
    greet([core, far] + [{"dp": peer_of(me, bit)[0]} for bit in sorted(set(firsts))])

    def post(kind, c, source, target, partner):
        return send(source, target, sems.at[0, kind, c], sems.at[1, kind, c], partner)

    att_copy = post(ATT, 0, att_ref.at[pl.ds(2, 2)], near, core)
    fetches = []
    for n, (source, target) in enumerate(
        [
            (win_hbm, win.at[0]),
            (win_near_hbm, win.at[1]),
            (wdn_hbm, wdn.at[pl.ds(0, hidden)]),
            (wdn_near_hbm, wdn.at[pl.ds(hidden, hidden)]),
        ]
    ):
        fetches.append(pltpu.make_async_copy(source, target, loads.at[n]))
        fetches[-1].start()
    sums[...] = jnp.zeros_like(sums)
    scale_one, shift_one, scale_two, shift_two = (ln_ref[i : i + 1, :] for i in range(4))
    att_copy.wait()

    def branch(index, where):
        return mm(att_ref[index, where, :], wo_ref[...]) + mm(near[index, where, :], wo_near_ref[...])

    def exchange(kind, value_of):
        copies = []
        for c, where in enumerate(chunks):
            outbox[where, :] = value_of(where).astype(BF16)
            copies.append(post(kind, c, outbox.at[where], inbox.at[where], far))
        return copies

    branch_copies = exchange(BRANCH, lambda where: branch(1, where))
    for where in chunks:
        hat[where, :] = tok_ref[where, :].astype(F32) + branch(0, where)

    def by_parts(c, part):
        step = 64

        def run(i, carry):
            part(pl.ds(pl.multiple_of(c * chunk + i * step, step), step))
            return carry

        lax.fori_loop(0, chunk // step, run, 0)

    def mean(values):
        return jnp.sum(values, axis=-1, keepdims=True) * (1.0 / width)

    def add_up(index, values):
        sums[index] += jnp.sum(values.reshape(values.shape[0] // 8, 8, width), axis=0)

    def norm_one(where):
        h = hat[where, :] + inbox[where, :].astype(F32)
        h = h - mean(h)
        r = lax.rsqrt(mean(h * h) + EPSILON)
        h = h * r
        hat[where, :] = h
        r1[where, :] = jnp.broadcast_to(r, (r.shape[0], LANES))
        h = h * scale_one + shift_one
        res[where, :] = h
        low[0, where, :] = h.astype(BF16)

    normed_copies = []
    for c, where in enumerate(chunks):
        branch_copies[c].wait()
        by_parts(c, norm_one)
        normed_copies.append(post(NORMED, c, low.at[0, where], low.at[1, where], far))
    for fetch in fetches:
        fetch.wait()

    tile = hidden // 2

    def mlp(side, where):
        def columns(t, carry):
            k, at = t // 2, (t % 2) * tile
            x = low[side, where, :]
            gate_at = pl.ds(pl.multiple_of(at, LANES), tile)
            up_at = pl.ds(pl.multiple_of(hidden + at, LANES), tile)
            gate, up = mm(x, win[k, :, gate_at]), mm(x, win[k, :, up_at])
            gu[side, k, where, gate_at] = gate.astype(BF16)
            gu[side, k, where, up_at] = up.astype(BF16)
            value = gate * jax.nn.sigmoid(gate) * up
            hid[side, where, pl.ds(pl.multiple_of(k * hidden + at, LANES), tile)] = value.astype(BF16)
            return carry

        lax.fori_loop(0, 4, columns, 0)
        return mm(hid[side, where, :], wdn[...])

    def both_sides(copies_in, kind, compute):
        copies = []
        for c, where in enumerate(chunks):
            own[where, :] = compute(0, where)
            copies_in[c].wait()
            outbox[where, :] = compute(1, where).astype(BF16)
            copies.append(post(kind, c, outbox.at[where], inbox.at[where], far))
        return copies

    out_copies = both_sides(normed_copies, OUT, mlp)

    def norm_two(where):
        z = res[where, :] + own[where, :] + inbox[where, :].astype(F32)
        z = z - mean(z)
        r = lax.rsqrt(mean(z * z) + EPSILON)
        z = z * r
        out_ref[where, :] = (z * scale_two + shift_two).astype(BF16)
        g = cot_ref[where, :].astype(F32)
        add_up(2, g * z)
        add_up(3, g)
        e = g * scale_two
        dz = r * (e - mean(e) - z * mean(e * z))
        res[where, :] = dz
        dlow[0, where, :] = dz.astype(BF16)

    dout_copies = []
    for c, where in enumerate(chunks):
        out_copies[c].wait()
        by_parts(c, norm_two)
        dout_copies.append(post(DOUT, c, dlow.at[0, where], dlow.at[1, where], far))

    def mlp_back(side, where):
        def columns(t, carry):
            k, at = t // 2, (t % 2) * tile
            d_hidden = mm(
                dlow[side, where, :], wdn[pl.ds(pl.multiple_of(k * hidden + at, LANES), tile), :], NT
            )
            gate_at = pl.ds(pl.multiple_of(at, LANES), tile)
            up_at = pl.ds(pl.multiple_of(hidden + at, LANES), tile)
            gate, up = gu[side, k, where, gate_at].astype(F32), gu[side, k, where, up_at].astype(F32)
            s = jax.nn.sigmoid(gate)
            gu[side, k, where, gate_at] = (d_hidden * up * s * (1.0 + gate * (1.0 - s))).astype(BF16)
            gu[side, k, where, up_at] = (d_hidden * gate * s).astype(BF16)
            return carry

        lax.fori_loop(0, 4, columns, 0)
        return mm(gu[side, 0, where, :], win[0], NT) + mm(gu[side, 1, where, :], win[1], NT)

    dnormed_copies = both_sides(dout_copies, DNORMED, mlp_back)

    def weight_grads(k, target):
        def chain(r, carry):
            at = pl.ds(pl.multiple_of(r * half, LANES), half)
            for n, place in enumerate((slice(0, hidden), slice(hidden, 2 * hidden))):
                piece = mm(low[0, :, at], gu[0, k, :, place], TN) + mm(low[1, :, at], gu[1, k, :, place], TN)
                target[r, n * half : (n + 1) * half, :] = piece.astype(target.dtype)
            at = pl.ds(pl.multiple_of(k * hidden + r * half, LANES), half)
            piece = mm(hid[0, :, at], dlow[0], TN) + mm(hid[1, :, at], dlow[1], TN)
            target[r, 2 * half : 3 * half, :] = piece.astype(target.dtype)
            return carry

        lax.fori_loop(0, 2, chain, 0)

    weight_grads(1, give)
    grad_copies = [post(GRAD_NEAR, r, give.at[r], take.at[r], core) for r in range(2)]

    def norm_one_back(where):
        d = res[where, :] + own[where, :] + inbox[where, :].astype(F32)
        h = hat[where, :]
        add_up(0, d * h)
        add_up(1, d)
        e = d * scale_one
        dh = r1[where, 0:1] * (e - mean(e) - h * mean(e * h))
        dh_ref[where, :] = dh
        slots_ref[0, where, :] = dh.astype(BF16)

    dh_copies, last_copies = [], []

    def dh_chunk(c):
        where = chunks[c]
        dnormed_copies[c].wait()
        by_parts(c, norm_one_back)
        mine = slots_ref.at[0, where]
        dh_copies.append(post(DH, c, mine, slots_ref.at[1, where], far))
        last_copies.append(post(DH_NEAR, c, mine, slots_ref.at[2, where], core))

    dh_chunk(0)
    weight_grads(0, total)
    dh_chunk(1)
    size_rows = total.shape[1] // 2
    dp_copies, keeps = [], []
    for r in range(2):
        grad_copies[r].wait()
        total[r] += take[r].astype(F32)
        partner, mine = peer_of(me, firsts[r])
        away = pl.ds(pl.multiple_of((1 - mine) * size_rows, 16), size_rows)
        keeps.append(pl.ds(pl.multiple_of(mine * size_rows, 16), size_rows))
        give[r, :size_rows, :] = total[r, away, :].astype(BF16)
        dp_copies.append(post(GRAD_DP, r, give.at[r, pl.ds(0, size_rows)], take_dp.at[r], {"dp": partner}))
    for c, where in enumerate(chunks):
        dh_copies[c].wait()
        last_copies.append(post(DH_LAST, c, slots_ref.at[1, where], slots_ref.at[3, where], core))
    for i in range(4):
        norms_ref[i : i + 1, :] = jnp.sum(sums[i], axis=0, keepdims=True)
    norms_ref[4:8, :] = jnp.zeros((4, width), F32)
    writes = []
    for r in range(2):
        dp_copies[r].wait()
        total[r, keeps[r], :] += take_dp[r].astype(F32)
        writes.append(pltpu.make_async_copy(total.at[r, keeps[r]], kept_hbm.at[r], stores.at[r]))
        writes[-1].start()
    for copy in last_copies + writes:
        copy.wait()


def middle(att, w_out, w_out_near, tokens, cotangent, norms, w_in, w_in_near, w_down, w_down_near):
    size = lax.axis_size("dp")
    shards, rows, cols = att.shape
    width = tokens.shape[1]
    hidden = w_down.shape[0]
    chain = 3 * width // 2
    vmem = pl.BlockSpec(memory_space=pltpu.VMEM)
    hbm = pl.BlockSpec(memory_space=pl.ANY)
    dma = pltpu.SemaphoreType.DMA
    return pl.pallas_call(
        functools.partial(middle_kernel, size),
        out_shape=(
            jax.ShapeDtypeStruct((rows, width), BF16),
            jax.ShapeDtypeStruct((rows, width), F32),
            jax.ShapeDtypeStruct((shards, rows, width), BF16),
            jax.ShapeDtypeStruct((8, width), F32),
            jax.ShapeDtypeStruct((2, chain // 2, width), F32),
        ),
        in_specs=[vmem] * 6 + [hbm] * 4,
        out_specs=[vmem] * 4 + [hbm],
        scratch_shapes=[
            pltpu.VMEM((2, width, 2 * hidden), BF16),
            pltpu.VMEM((2 * hidden, width), BF16),
            pltpu.VMEM((2, rows, cols), BF16),
            pltpu.VMEM((rows, width), BF16),
            pltpu.VMEM((rows, width), BF16),
            pltpu.VMEM((2, rows, width), BF16),
            pltpu.VMEM((rows, width), F32),
            pltpu.VMEM((rows, width), F32),
            pltpu.VMEM((rows, width), F32),
            pltpu.VMEM((rows, LANES), F32),
            pltpu.VMEM((2, 2, rows, 2 * hidden), BF16),
            pltpu.VMEM((2, rows, 2 * hidden), BF16),
            pltpu.VMEM((2, rows, width), BF16),
            pltpu.VMEM((2, chain, width), F32),
            pltpu.VMEM((2, chain, width), BF16),
            pltpu.VMEM((2, chain, width), BF16),
            pltpu.VMEM((2, chain // 2, width), BF16),
            pltpu.VMEM((4, 8, width), F32),
            dma((2, 11, 2)),
            dma((4,)),
            dma((2,)),
        ],
        compiler_params=pltpu.CompilerParams(
            collective_id=0, has_side_effects=True, vmem_limit_bytes=WIDE_LIMIT
        ),
        cost_estimate=pl.CostEstimate(
            flops=36 * rows * width * hidden, bytes_accessed=40 * rows * width, transcendentals=0
        ),
        name="middle",
    )(att, w_out, w_out_near, tokens, cotangent, norms, w_in, w_in_near, w_down, w_down_near)


class Sum:
    def __init__(self, size, me, first, total, give, take, result, sems):
        orders = dp_orders(size)
        self.total, self.give, self.take, self.result, self.sems = total, give, take, result, sems
        halving, stages = halvings(size), size.bit_length() - 1
        count = 1 << (halving - first)
        self.rows = total.shape[1] // count
        base, low, peers = [], [0, 0], []
        for chain in range(2):
            peers.append([peer_of(me, bit) for bit in orders[chain]])
            base.append(sum(peers[chain][done][1] * (1 << (halving - 1 - done)) for done in range(first)))
        self.steps, spot = [], 0
        for stage in range(first, stages):
            halve = stage < halving
            part = count // 2 if halve else count
            step = dict(kind="halve" if halve else "swap", part=part, spot=spot, chains=[], last=stage + 1 == stages)
            for chain in range(2):
                peer, mine = peers[chain][stage]
                away = low[chain] + (1 - mine) * part if halve else low[chain]
                low[chain] = low[chain] + mine * part if halve else low[chain]
                step["chains"].append(dict(peer=peer, away=away, keep=low[chain], final=base[chain] + low[chain]))
            self.steps.append(step)
            spot, count = spot + part, part
        low = [base[chain] + low[chain] for chain in range(2)]
        for stage in reversed(range(halving)):
            step = dict(kind="gather", part=count, chains=[])
            for chain in range(2):
                peer, mine = peers[chain][stage]
                step["chains"].append(dict(peer=peer, away=low[chain]))
                low[chain] = low[chain] - mine * count
            self.steps.append(step)
            count *= 2

    def block(self, low, count):
        return pl.ds(pl.multiple_of(low * self.rows, 16), count * self.rows)

    def copy(self, index, chain):
        step = self.steps[index]
        one = step["chains"][chain]
        if step["kind"] == "gather":
            source = target = self.result.at[chain, self.block(one["away"], step["part"])]
        else:
            spot = pl.ds(step["spot"] * self.rows, step["part"] * self.rows)
            source, target = self.give.at[chain, spot], self.take.at[chain, spot]
        return pltpu.make_async_remote_copy(
            source,
            target,
            self.sems.at[0, chain, index],
            self.sems.at[1, chain, index],
            device_id={"dp": one["peer"]},
            device_id_type=MESH,
        )

    def start(self, index):
        step = self.steps[index]
        for chain in range(2):
            if step["kind"] != "gather":
                spot = pl.ds(step["spot"] * self.rows, step["part"] * self.rows)
                away = self.block(step["chains"][chain]["away"], step["part"])
                self.give[chain, spot, :] = self.total[chain, away, :].astype(BF16)
            self.copy(index, chain).start()

    def finish(self, index):
        step = self.steps[index]
        for chain in range(2):
            self.copy(index, chain).wait()
            if step["kind"] == "gather":
                continue
            one = step["chains"][chain]
            spot = pl.ds(step["spot"] * self.rows, step["part"] * self.rows)
            keep = self.block(one["keep"], step["part"])
            mine = self.total[chain, keep, :] if step["kind"] == "halve" else self.give[chain, spot, :].astype(F32)
            value = mine + self.take[chain, spot, :].astype(F32)
            if step["last"]:
                self.result[chain, self.block(one["final"], 1), :] = value.astype(BF16)
            else:
                self.total[chain, keep, :] = value

    def advance(self, index):
        self.finish(index)
        if index + 1 < len(self.steps):
            self.start(index + 1)


def pieces_sent(size, first):
    halving = halvings(size)
    return (1 << (halving - first)) - 1 + size.bit_length() - 1 - halving


def back_kernel(
    size, att_ref, w_out_ref, cos_ref, sin_ref, norms_ref, w_ref, w_near_ref, dh_ref,
    kept_hbm, slots_hbm, q_rows_hbm, q_hbm, k_hbm, v_hbm, x_hbm,
    dx_ref, grad_ref, big_ref, sums_ref,
    big, slots, q_rows_ref, q_ref, k_ref, v_ref, x_ref,
    do_ref, do_rows_ref, dq_ref, dk_ref, dv_ref, d_qkv,
    total, give, take, big_give, big_take, near, far_out, far_in, own, norm_in,
    loads, near_sem, far_sem, sum_sems, big_sems, norm_sem,
):
    heads, _, tokens = k_ref.shape
    shards, rows, width = slots.shape
    cols = heads * HEAD_DIM
    half = HEAD_DIM // 2
    m, me = lax.axis_index("mp"), lax.axis_index("dp")
    stages = size.bit_length() - 1
    core, far = {"mp": peer_of(m, 0)[0]}, {"mp": peer_of(m, 1)[0]}
    partners = [core, far] + [{"dp": peer_of(me, bit)[0]} for bit in range(stages)]
    sources = [kept_hbm, slots_hbm, q_rows_hbm, q_hbm, k_hbm, v_hbm, x_hbm]
    targets = [big, slots, q_rows_ref, q_ref, k_ref, v_ref, x_ref]
    fetches = [
        pltpu.make_async_copy(source, target, loads.at[n])
        for n, (source, target) in enumerate(zip(sources, targets))
    ]
    for fetch in fetches:
        fetch.start()
    greet(partners)
    sums_ref[...] = norms_ref[...]
    large = Sum(size, me, 1, big, big_give, big_take, big_ref, big_sems)
    small = Sum(size, me, 0, total, give, take, grad_ref, sum_sems)
    fetches[0].wait()
    large.start(0)
    fetches[1].wait()

    def slot_at(shard):
        return (shard // 2 + m // 2) % 2 + 2 * ((shard + m) % 2)

    def shard_at(slot):
        return 2 * ((slot % 2 + m // 2) % 2) + (slot // 2 + m) % 2

    def prepare(i, carry):
        d_att = mm(w_out_ref[...], slots[slot_at(i)], NT).astype(BF16)
        do_ref[:, span(i, rows)] = d_att
        products = d_att.astype(F32) * att_ref[:, span(i, rows)].astype(F32)
        for h in range(heads):
            mine = slice(h * HEAD_DIM, (h + 1) * HEAD_DIM)
            dot = jnp.sum(products[mine], axis=0, keepdims=True)
            wide = [d_att[mine].astype(F32), thirds(-dot), jnp.zeros((LANES - HEAD_DIM - 16, rows), F32)]
            do_rows_ref[h, span(i, rows), :] = jnp.concatenate(wide, axis=0).T.astype(BF16)
        return carry

    lax.fori_loop(0, shards, prepare, 0)
    dq_ref[...] = jnp.zeros_like(dq_ref)
    for fetch in fetches[2:]:
        fetch.wait()

    def rotated_back(values, cosine, sine):
        first, second = values[:half], values[half:]
        return [first * cosine + second * sine, second * cosine - first * sine]

    def over_keys(j, carry):
        keys = span(j, rows)
        dk_ref[...] = jnp.zeros_like(dk_ref)
        dv_ref[...] = jnp.zeros_like(dv_ref)

        def over_queries(i, carry):
            queries = span(i, rows)
            for h in range(heads):
                k = k_ref[h, :, keys]
                probs = jnp.exp2(mm(q_rows_ref[h, queries, :], k))
                d_scores = (probs * mm(do_rows_ref[h, queries, :], v_ref[h, :, keys])).astype(BF16)
                dv_ref[h] += mm(do_ref[h * HEAD_DIM : (h + 1) * HEAD_DIM, queries], probs.astype(BF16))
                dk_ref[h] += mm(q_ref[h, :HEAD_DIM, queries], d_scores)
                dq_ref[h, :, queries] += mm(k[:HEAD_DIM], d_scores, NT)
            return carry

        lax.fori_loop(0, shards, over_queries, 0)
        cosine, sine = cos_ref[:, keys] * (1.0 / LOG2E), sin_ref[:, keys] * (1.0 / LOG2E)
        pieces = []
        for h in range(heads):
            pieces += rotated_back(dk_ref[h], cosine, sine)
        pieces += [dv_ref[h] for h in range(heads)]
        d_qkv[slot_at(j), cols:, :] = jnp.concatenate(pieces, axis=0).astype(BF16)
        for index, when in enumerate((0, 2)):
            pl.when(j == when)(lambda index=index: large.advance(index))
        return carry

    lax.fori_loop(0, shards, over_keys, 0)
    done = 2
    for i in range(shards):
        scale = 1.0 / math.sqrt(HEAD_DIM)
        cosine, sine = cos_ref[:, span(i, rows)] * scale, sin_ref[:, span(i, rows)] * scale
        pieces = []
        for h in range(heads):
            pieces += rotated_back(dq_ref[h, :, span(i, rows)], cosine, sine)
        d_qkv[slot_at(i), :cols, :] = jnp.concatenate(pieces, axis=0).astype(BF16)
    near_copy = send(d_qkv.at[pl.ds(2, 2)], near, near_sem.at[0], near_sem.at[1], core)

    def product(first, count):
        piece = mm(d_qkv[0, first : first + count, :], x_ref[0])
        for slot in range(1, shards):
            piece += mm(d_qkv[slot, first : first + count, :], x_ref[slot])
        return piece

    chain_rows = total.shape[1]
    total[0] = product(0, chain_rows)
    total[1, :cols, :] = product(chain_rows, cols)
    piece = mm(att_ref[:, span(shard_at(0), rows)], slots[0])
    for slot in range(1, shards):
        piece += mm(att_ref[:, span(shard_at(slot), rows)], slots[slot])
    total[1, cols:, :] = piece
    small.start(0)

    def norm_exchange(stage):
        return send(sums_ref, norm_in.at[stage], norm_sem.at[0, stage], norm_sem.at[1, stage], partners[stage])

    norm_copy, norm_done = norm_exchange(0), 0
    near_copy.wait()

    def d_tokens(index):
        return mm(d_qkv[index], w_ref[...], TN) + mm(near[index], w_near_ref[...], TN)

    far_out[...] = d_tokens(1).astype(BF16)
    far_copy = send(far_out, far_in, far_sem.at[0], far_sem.at[1], far)
    own[...] = dh_ref[...] + d_tokens(0)

    small_done = 0
    while done < len(large.steps) or small_done < len(small.steps) or norm_done < len(partners):
        if small_done < len(small.steps):
            small.advance(small_done)
            small_done += 1
        if done < len(large.steps):
            large.advance(done)
            done += 1
        if norm_done < len(partners):
            norm_copy.wait()
            sums_ref[...] += norm_in[norm_done]
            norm_done += 1
            if norm_done < len(partners):
                norm_copy = norm_exchange(norm_done)
    far_copy.wait()
    dx_ref[...] = (own[...] + far_in[...].astype(F32)).astype(BF16)


def back(att_along, w_out, cosine, sine, norms, w_turned, w_near, dh, kept, dh_slots, q_rows, q, k, v, x_slots):
    size = lax.axis_size("dp")
    stages = size.bit_length() - 1
    heads, _, tokens = q.shape
    shards, rows, width = x_slots.shape
    cols = w_turned.shape[0]
    chain, big_chain = width // 2, kept.shape[1] * 2
    sent = pieces_sent(size, 0) * (chain >> halvings(size))
    big_sent = pieces_sent(size, 1) * (big_chain >> halvings(size))
    steps = stages + halvings(size)
    vmem = pl.BlockSpec(memory_space=pltpu.VMEM)
    hbm = pl.BlockSpec(memory_space=pl.ANY)
    dma = pltpu.SemaphoreType.DMA
    along = pltpu.VMEM((heads, LANES, tokens), BF16)
    return pl.pallas_call(
        functools.partial(back_kernel, size),
        out_shape=(
            jax.ShapeDtypeStruct((rows, width), BF16),
            jax.ShapeDtypeStruct((2, chain, width), BF16),
            jax.ShapeDtypeStruct((2, big_chain, width), BF16),
            jax.ShapeDtypeStruct(norms.shape, F32),
        ),
        in_specs=[vmem] * 8 + [hbm] * 7,
        out_specs=[vmem] * 4,
        scratch_shapes=[
            pltpu.VMEM(kept.shape, F32),
            pltpu.VMEM(dh_slots.shape, BF16),
            pltpu.VMEM((heads, tokens, LANES), BF16),
            along,
            along,
            along,
            pltpu.VMEM(x_slots.shape, BF16),
            pltpu.VMEM((heads * HEAD_DIM, tokens), BF16),
            pltpu.VMEM((heads, tokens, LANES), BF16),
            pltpu.VMEM((heads, HEAD_DIM, tokens), F32),
            pltpu.VMEM((heads, HEAD_DIM, rows), F32),
            pltpu.VMEM((heads, HEAD_DIM, rows), F32),
            pltpu.VMEM((shards, cols, rows), BF16),
            pltpu.VMEM((2, chain, width), F32),
            pltpu.VMEM((2, sent, width), BF16),
            pltpu.VMEM((2, sent, width), BF16),
            pltpu.VMEM((2, big_sent, width), BF16),
            pltpu.VMEM((2, big_sent, width), BF16),
            pltpu.VMEM((2, cols, rows), BF16),
            pltpu.VMEM((rows, width), BF16),
            pltpu.VMEM((rows, width), BF16),
            pltpu.VMEM((rows, width), F32),
            pltpu.VMEM((2 + stages,) + norms.shape, F32),
            dma((7,)),
            dma((2,)),
            dma((2,)),
            dma((2, 2, steps)),
            dma((2, 2, steps)),
            dma((2, 2 + stages)),
        ],
        compiler_params=pltpu.CompilerParams(
            collective_id=1, has_side_effects=True, vmem_limit_bytes=WIDE_LIMIT
        ),
        cost_estimate=pl.CostEstimate(
            flops=5 * heads * tokens * tokens * LANES, bytes_accessed=60 * rows * width, transcendentals=0
        ),
        name="back",
    )(att_along, w_out, cosine, sine, norms, w_turned, w_near, dh, kept, dh_slots, q_rows, q, k, v, x_slots)


def emit_kernel(big_ref, small_ref, gate_up_ref, down_ref, qkv_ref, out_ref):
    for n in range(2):
        gate_up_ref[:, n, :] = big_ref[0, n].astype(F32)
    down_ref[...] = big_ref[0, 2].astype(F32)
    qkv_steps = pl.num_programs(0) * 3 // 4

    @pl.when(pl.program_id(0) < qkv_steps)
    def _():
        qkv_ref[...] = small_ref[0].astype(F32)

    @pl.when(pl.program_id(0) >= qkv_steps)
    def _():
        out_ref[...] = small_ref[0].astype(F32)


def emit(big, small):
    _, chain, width = small.shape
    steps = 8
    per, rows = steps // 2, width // steps
    qkv_steps = steps * 3 // 4
    shape = lambda *dims: jax.ShapeDtypeStruct(dims, F32)
    return pl.pallas_call(
        emit_kernel,
        out_shape=(
            shape(width, 2, width),
            shape(width, width),
            shape(qkv_steps * rows, width),
            shape((steps - qkv_steps) * rows, width),
        ),
        grid=(steps,),
        in_specs=[
            pl.BlockSpec((1, 3, rows, width), lambda i: (i // per, 0, i % per, 0)),
            pl.BlockSpec((1, rows, width), lambda i: (i // per, i % per, 0)),
        ],
        out_specs=[
            pl.BlockSpec((rows, 2, width), lambda i: (i, 0, 0)),
            pl.BlockSpec((rows, width), lambda i: (i, 0)),
            pl.BlockSpec((rows, width), lambda i: (jnp.minimum(i, qkv_steps - 1), 0)),
            pl.BlockSpec((rows, width), lambda i: (jnp.maximum(i - qkv_steps, 0), 0)),
        ],
        compiler_params=pltpu.CompilerParams(vmem_limit_bytes=VMEM_LIMIT),
        cost_estimate=pl.CostEstimate(flops=0, bytes_accessed=24 * width * width, transcendentals=0),
        name="emit",
    )(big.reshape(2, 3, chain, width), small)


def body(
    tokens, lengths, w_qkv, w_out, w_gate_up, w_down, ln1_scale, ln1_shift, ln2_scale, ln2_shift, cotangent
):
    rows, width = tokens.shape
    shards = lax.axis_size("mp")
    length = rows * shards
    local_cols = w_out.shape[0]
    heads = local_cols // HEAD_DIM
    hidden_cols = w_down.shape[0]
    m = lax.axis_index("mp")

    def swap(values, distance):
        return lax.ppermute(values, "mp", [(i, i ^ distance) for i in range(shards)])

    across = lambda values: swap(values, 2)
    beside = lambda values: swap(values, 1)

    x_far = across(tokens)
    x_near = beside(tokens)
    x_last = beside(x_far)
    positions, key_tiles, bounds = doc_tables(lengths[0], length, rows)
    cosine, sine = rotary(positions)
    place = jnp.stack([m.astype(jnp.int32)] + [jnp.int32(r) for r in (0, 2, 1, 3)])
    qkv_turned = w_qkv.transpose(1, 2, 0).reshape(3 * local_cols, width)
    qkv_near = beside(qkv_turned)
    w_out_near = beside(w_out)
    flat_gate_up = w_gate_up.reshape(width, 2 * hidden_cols)
    w_gate_up_near = beside(flat_gate_up)
    w_down_near = beside(w_down)
    x_slots = jnp.stack([tokens, x_far, x_near, x_last])
    q, k, v, k_rows = project(x_slots, qkv_turned, cosine, sine, bounds, place, heads)
    att, att_along, q_rows = attend(q, k_rows, v, place, key_tiles, shards)
    norms = jnp.concatenate([jnp.stack([ln1_scale, ln1_shift, ln2_scale, ln2_shift]), jnp.zeros((4, width), F32)])
    output, dh, dh_slots, norms, kept = middle(
        att, w_out, w_out_near, tokens, cotangent, norms, flat_gate_up, w_gate_up_near, w_down, w_down_near
    )
    d_tokens, small, big, norms = back(
        att_along, w_out, cosine, sine, norms, qkv_turned, qkv_near, dh, kept, dh_slots, q_rows, q, k, v, x_slots
    )
    grad_gate_up, grad_down, grad_qkv, grad_out = emit(big, small)
    grad_qkv = grad_qkv.reshape(3, local_cols, width).transpose(2, 0, 1)
    norms = lax.dynamic_slice_in_dim(norms, m * local_cols, local_cols, 1)
    return (
        output,
        d_tokens,
        grad_qkv,
        grad_out,
        grad_gate_up,
        grad_down,
        norms[0],
        norms[1],
        norms[2],
        norms[3],
    )


def solution(mesh):
    return jax.shard_map(
        body,
        mesh=mesh,
        in_specs=(
            P(("dp", "mp"), None),
            P("dp", None),
            P(None, None, "mp"),
            P("mp", None),
            P(None, None, "mp"),
            P("mp", None),
            P(),
            P(),
            P(),
            P(),
            P(("dp", "mp"), None),
        ),
        out_specs=(
            P(("dp", "mp"), None),
            P(("dp", "mp"), None),
            P(None, None, "mp"),
            P("mp", None),
            P(None, None, "mp"),
            P("mp", None),
            P("mp"),
            P("mp"),
            P("mp"),
            P("mp"),
        ),
        check_vma=False,
    )
```

profile of v0, /device:TPU:0, one launch (start us, length us, event | category | flops | bytes accessed | tf_op | source)
XLA Modules:
  0.0 307.1 jit_solution(2842150609574093156)
XLA Ops:
  0.6 3.0 collective-permute-start
  3.7 0.0 collective-permute-start.1
  3.7 0.0 copy-start.5
  3.7 0.0 copy-start.6
  3.7 0.0 copy-start.7
  3.7 0.0 copy-start.1
  3.7 2.2 copy.32
  5.9 0.0 copy-start
  5.9 0.6 collective-permute-start.4
  6.5 0.1 collective-permute-start.5
  6.6 0.0 copy-done.9
  6.6 0.4 collective-permute-start.3
  7.0 0.0 copy-done.8
  7.0 0.1 copy.30
  7.1 0.1 fusion.3
  7.2 0.7 pad_add_fusion.bounds_ref
  7.9 0.0 copy-done.4
  7.9 0.0 copy-done.5
  8.0 0.0 copy-done.6
  8.0 0.0 copy-done.7
  8.0 0.6 stack.43.place
  8.6 0.6 concatenate.7.ln_ref
  9.3 0.2 select_reduce_fusion.2
  9.5 0.1 select_reduce_fusion
  9.6 11.9 %collective-permute-done = bf16[512,768]{1,0:T(8,128)(2,1)} collective-permute-done((bf16[512,768]{1,0:T(8,128)(2,1)}, bf16[512,768]{1,0:T(8,128)(2,1)}, u32[]{:S(2)}, u32[]{:S(2)}) %collective-permute-start) | collective-permute-done | bytes 786464 | tf_op jit(solution)/shard_map/ppermute | solution.py:860
  21.5 0.0 collective-permute-start.2
  21.5 0.6 pad_add_fusion.1.ranges
  22.1 1.8 multiply_sine_fusion
  23.9 0.0 collective-permute-done.1
  23.9 0.5 collective-permute-start.6
  24.4 0.0 collective-permute-done.2
  24.4 0.0 copy-done.1
  24.4 3.0 pad_maximum_fusion.x_ref.x_hbm
  27.4 0.0 copy-done
  27.4 7.5 %project.1 = (bf16[3,128,2048]{2,1,0:T(8,128)(2,1)}, bf16[3,128,2048]{2,1,0:T(8,128)(2,1)}, bf16[3,128,2048]{2,1,0:T(8,128)(2,1)}, bf16[3,2048,128]{2,1,0:T(8,128)(2,1)}) custom-call(s32[5]{0:T(128)} %stack.43.place, bf16[4,512,768]{2,1,0:T(8,128)(2,1)} %pad_maximum_fusion.x_ref.x_hbm, bf16[576,768]{1,0:T(8,128)(2,1)} %bitcast.38, ...), custom_call_target="tpu_custom_call" | custom-call | flops 1811939328 | bytes 9437184 | tf_op jit(solution)/shard_map/project/pallas_call | solution.py:87
  34.9 23.2 %attend.1 = (bf16[4,512,192]{2,1,0:T(8,128)(2,1)}, bf16[192,2048]{1,0:T(8,128)(2,1)}, bf16[3,2048,128]{2,1,0:T(8,128)(2,1)}) custom-call(s32[5]{0:T(128)} %stack.43.place, s32[8]{0:T(128)} %pad_add_fusion.1.ranges, bf16[3,128,2048]{2,1,0:T(8,128)(2,1)} %get-tuple-element.30.q_ref.q_hbm, bf16[3,2048,128]{2,1,0:T(8,128)(2,1)} %get-tuple-element.31.k_ref, ...), custom_call_target="tpu_custom_call" | custom-call | flops 3221225472 | bytes 7864320 | tf_op jit(solution)/shard_map/attend/pallas_call | solution.py:146
  58.1 0.0 collective-permute-done.3.wo_near_ref
  58.1 0.0 collective-permute-done.5.wdn_near_hbm
  58.1 0.0 collective-permute-done.4.win_near_hbm
  58.2 120.0 %middle.1 = (bf16[512,768]{1,0:T(8,128)(2,1)}, f32[512,768]{1,0:T(8,128)}, bf16[4,512,768]{2,1,0:T(8,128)(2,1)}, f32[8,768]{1,0:T(8,128)}, f32[2,576,768]{2,1,0:T(8,128)}) custom-call(bf16[4,512,192]{2,1,0:T(8,128)(2,1)} %get-tuple-element.33.att_ref, bf16[192,768]{1,0:T(8,128)(2,1)} %w_out_ref.1, bf16[192,768]{1,0:T(8,128)(2,1)} %collective-permute-done.3.wo_near_ref, ...), custom_call_target="tpu_custom_call" | custom-call | flops 10871635968 | bytes 15728640 | tf_op jit(solution)/shard_map/middle/pallas_call | solution.py:461
  178.2 0.0 collective-permute-done.6.w_near_ref
  178.2 117.3 %back.1 = (bf16[512,768]{1,0:T(8,128)(2,1)}, bf16[2,384,768]{2,1,0:T(8,128)(2,1)}, bf16[2,1152,768]{2,1,0:T(8,128)(2,1)}, f32[8,768]{1,0:T(8,128)}) custom-call(bf16[192,2048]{1,0:T(8,128)(2,1)} %get-tuple-element.35.att_ref, bf16[192,768]{1,0:T(8,128)(2,1)} %w_out_ref.1, f32[32,2048]{1,0:T(8,128)} %get-tuple-element.57.cos_ref, ...), custom_call_target="tpu_custom_call" | custom-call | flops 8053063680 | bytes 23592960 | tf_op jit(solution)/shard_map/back/pallas_call | solution.py:751
  295.5 0.0 copy-start.2
  295.5 8.3 %emit.1 = (f32[768,2,768]{2,1,0:T(2,128)}, f32[768,768]{1,0:T(8,128)}, f32[576,768]{1,0:T(8,128)}, f32[192,768]{1,0:T(8,128)}) custom-call(bf16[2,3,384,768]{3,2,1,0:T(8,128)(2,1)} %bitcast.25, bf16[2,384,768]{2,1,0:T(8,128)(2,1)} %get-tuple-element.44.small_ref), custom_call_target="tpu_custom_call" | custom-call | bytes 14155776 | tf_op jit(solution)/shard_map/emit/pallas_call | solution.py:823
  303.8 1.5 fusion.2
  305.3 0.9 copy.35
  306.2 0.0 copy-done.3
  306.2 0.9 copy.36
  (17 shorter events, 0.1 us)
Async XLA Ops:
  0.6 20.9 %collective-permute-start = (bf16[512,768]{1,0:T(8,128)(2,1)}, bf16[512,768]{1,0:T(8,128)(2,1)}, u32[]{:S(2)}, u32[]{:S(2)}) collective-permute-start(bf16[512,768]{1,0:T(8,128)(2,1)} %tok_ref.1), channel_id=1, source_target_pairs={{0,2},{1,3},{2,0},{3,1},{4,6},{5,7},{6,4},{7,5},{8,10},{9,11},{10,... | collective-permute-start | bytes 2359304 | tf_op jit(solution)/shard_map/ppermute | solution.py:860
  3.7 20.2 %collective-permute-start.1 = (bf16[512,768]{1,0:T(8,128)(2,1)}, bf16[512,768]{1,0:T(8,128)(2,1)}, u32[]{:S(2)}, u32[]{:S(2)}) collective-permute-start(bf16[512,768]{1,0:T(8,128)(2,1)} %tok_ref.1), channel_id=1, source_target_pairs={{0,1},{1,0},{2,3},{3,2},{4,5},{5,4},{6,7},{7,6},{8,9},{9,8},{10,11... | collective-permute-start | bytes 2359304 | tf_op jit(solution)/shard_map/ppermute | solution.py:860
  3.7 2.9 copy-start.9
  3.7 3.3 %copy-start.8 = (s32[1,16]{1,0:T(1,128)S(1)}, s32[1,16]{1,0:T(1,128)}, u32[]{:S(2)}) copy-start(s32[1,16]{1,0:T(1,128)} %param.12) | copy-start | bytes 196
  3.7 4.2 %copy-start.4 = (f32[768]{0:T(1024)S(1)}, f32[768]{0:T(1024)}, u32[]{:S(2)}) copy-start(f32[768]{0:T(1024)} %param.17) | copy-start | bytes 9220
  3.7 4.3 %copy-start.5 = (f32[768]{0:T(1024)S(1)}, f32[768]{0:T(1024)}, u32[]{:S(2)}) copy-start(f32[768]{0:T(1024)} %param.18) | copy-start | bytes 9220
  3.7 4.3 %copy-start.6 = (f32[768]{0:T(1024)S(1)}, f32[768]{0:T(1024)}, u32[]{:S(2)}) copy-start(f32[768]{0:T(1024)} %param.19) | copy-start | bytes 9220
  3.7 4.3 %copy-start.7 = (f32[768]{0:T(1024)S(1)}, f32[768]{0:T(1024)}, u32[]{:S(2)}) copy-start(f32[768]{0:T(1024)} %param.20) | copy-start | bytes 9220
  3.7 20.7 %copy-start.1 = (bf16[512,768]{1,0:T(8,128)(2,1)S(1)}, bf16[512,768]{1,0:T(8,128)(2,1)}, u32[]{:S(2)}) copy-start(bf16[512,768]{1,0:T(8,128)(2,1)} %tok_ref.1) | copy-start | bytes 2359300
  5.9 21.5 %copy-start = (bf16[96,8,2,768]{3,1,2,0:T(8,128)(2,1)}, bf16[96,8,2,768]{3,1,2,0:T(8,128)(2,1)S(1)}, u32[]{:S(2)}) copy-start(bf16[96,8,2,768]{3,1,2,0:T(8,128)(2,1)S(1)} %copy.32) | copy-start | bytes 7077892
  5.9 52.2 %collective-permute-start.4 = (bf16[768,1536]{1,0:T(8,128)(2,1)S(1)}, bf16[768,1536]{1,0:T(8,128)(2,1)}, u32[]{:S(2)}, u32[]{:S(2)}) collective-permute-start(bf16[768,1536]{1,0:T(8,128)(2,1)S(1)} %bitcast.27), channel_id=1, source_target_pairs={{0,1},{1,0},{2,3},{3,2},{4,5},{5,4},{6,7},{7,6},{8,9},{9,8},{10,11... | collective-permute-start | bytes 7077896 | tf_op jit(solution)/shard_map/ppermute | solution.py:860
  6.5 51.6 %collective-permute-start.5 = (bf16[768,768]{1,0:T(8,128)(2,1)}, bf16[768,768]{1,0:T(8,128)(2,1)}, u32[]{:S(2)}, u32[]{:S(2)}) collective-permute-start(bf16[768,768]{1,0:T(8,128)(2,1)} %wdn_hbm.1), channel_id=1, source_target_pairs={{0,1},{1,0},{2,3},{3,2},{4,5},{5,4},{6,7},{7,6},{8,9},{9,8},{10,11... | collective-permute-start | bytes 3538952 | tf_op jit(solution)/shard_map/ppermute | solution.py:860
  6.6 51.6 %collective-permute-start.3 = (bf16[192,768]{1,0:T(8,128)(2,1)S(1)}, bf16[192,768]{1,0:T(8,128)(2,1)}, u32[]{:S(2)}, u32[]{:S(2)}) collective-permute-start(bf16[192,768]{1,0:T(8,128)(2,1)S(1)} %copy-done.9), channel_id=1, source_target_pairs={{0,1},{1,0},{2,3},{3,2},{4,5},{5,4},{6,7},{7,6},{8,9},{9,8},{10,11... | collective-permute-start | bytes 884744 | tf_op jit(solution)/shard_map/ppermute | solution.py:860
  21.5 2.9 collective-permute-start.2
  23.9 154.3 %collective-permute-start.6 = (bf16[576,768]{1,0:T(8,128)(2,1)}, bf16[576,768]{1,0:T(8,128)(2,1)}, u32[]{:S(2)}, u32[]{:S(2)}) collective-permute-start(bf16[576,768]{1,0:T(8,128)(2,1)} %bitcast.37), channel_id=1, source_target_pairs={{0,1},{1,0},{2,3},{3,2},{4,5},{5,4},{6,7},{7,6},{8,9},{9,8},{10,11... | collective-permute-start | bytes 2654216 | tf_op jit(solution)/shard_map/ppermute | solution.py:860
  295.5 9.8 %copy-start.2 = (bf16[512,768]{1,0:T(8,128)(2,1)S(1)}, bf16[512,768]{1,0:T(8,128)(2,1)}, u32[]{:S(2)}) copy-start(bf16[512,768]{1,0:T(8,128)(2,1)} %get-tuple-element.72) | copy-start | bytes 2359300
  295.5 10.7 %copy-start.3 = (bf16[512,768]{1,0:T(8,128)(2,1)S(1)}, bf16[512,768]{1,0:T(8,128)(2,1)}, u32[]{:S(2)}) copy-start(bf16[512,768]{1,0:T(8,128)(2,1)} %get-tuple-element.73) | copy-start | bytes 2359300
where the time goes:
time: 308 us; the launch traced here: 307 us
  Pallas kernels  276 us (90%)
  waiting for transfers between devices  11.9 us (4%)
  local copies, waits for them, and re-layouts  6.83 us (2%)
  other arithmetic  6.54 us (2%)
  starting transfers between devices  4.62 us (2%)
    pallas_call x1, Pallas kernels, middle(): pl.pallas_call(functools.partial(middle_kernel, size), out_shape=(jax.Sha...  120 us
    pallas_call x1, Pallas kernels, back(): pl.pallas_call(functools.partial(back_kernel, size), out_shape=(jax.Shape...  117 us
    pallas_call x1, Pallas kernels, attend(): pl.pallas_call(attend_kernel, out_shape=(jax.ShapeDtypeStruct((shards, ro...  23.2 us
    ppermute x7, waiting for transfers between devices, swap(): lax.ppermute(values, 'mp', [(i, i ^ distance) for i in range(shards)])  11.9 us
    pallas_call x1, Pallas kernels, emit(): pl.pallas_call(emit_kernel, out_shape=(shape(width, 2, width), shape(widt...  8.3 us
    pallas_call x1, Pallas kernels, project(): pl.pallas_call(project_kernel, out_shape=(along, along, along, down), gri...  7.53 us
  transfers between devices with their start and end apart: 7, of which 1 were waited for; matrix products, arithmetic and copies ran while one was open for 3% of the time, Pallas kernels for 49%

commit v1 on v0

v1 whole, which is shorter than its diff:
```python
import functools
import math

import jax
import jax.numpy as jnp
from jax import lax
from jax.experimental import pallas as pl
from jax.experimental.pallas import tpu as pltpu
from jax.sharding import PartitionSpec as P

F32 = jnp.float32
BF16 = jnp.bfloat16
HEAD_DIM = 64
LANES = 128
EPSILON = 1e-05
FAR = -(2.0**100)
LOG2E = math.log2(math.e)
NT = (((1,), (1,)), ((), ()))
TN = (((0,), (0,)), ((), ()))
NN = (((1,), (0,)), ((), ()))
VMEM_LIMIT = 58 << 20
WIDE_LIMIT = 62 << 20
MESH = pl.DeviceIdType.MESH


def mm(a, b, dims=NN):
    return lax.dot_general(a, b, dims, preferred_element_type=F32)


def thirds(row):
    high = row.astype(BF16).astype(F32)
    mid = (row - high).astype(BF16).astype(F32)
    low = row - high - mid
    return jnp.concatenate([high, mid, low, jnp.zeros((13, row.shape[1]), F32)], axis=0)


def span(index, size):
    if isinstance(index, int):
        return pl.ds(index * size, size)
    return pl.ds(pl.multiple_of(index * size, size), size)


def dp_orders(size):
    bits = list(range(size.bit_length() - 1))
    return [bits, bits[1::-1] + bits[2:]]


def halvings(size):
    return min(3, size.bit_length() - 1)


def peer_of(index, bit):
    mine = (index // (1 << bit)) % 2
    return index + (1 - 2 * mine) * (1 << bit), mine


def send(source, target, send_sem, recv_sem, partner):
    copy = pltpu.make_async_remote_copy(
        source, target, send_sem, recv_sem, device_id=partner, device_id_type=MESH
    )
    copy.start()
    return copy


def greet(partners):
    barrier = pltpu.get_barrier_semaphore()
    for partner in partners:
        pl.semaphore_signal(barrier, inc=1, device_id=partner, device_id_type=MESH)
    pl.semaphore_wait(barrier, len(partners))


RING_PIECES = 8
RING_EARLY = 2


class Ring:
    def __init__(self, size, me, total, give, take, result, scatter_sems, gather_sems):
        self.n = n = min(RING_PIECES, size)
        self.me, self.size = me, size
        self.total, self.give, self.take, self.result = total, give, take, result
        self.scatter_sems, self.gather_sems = scatter_sems, gather_sems
        self.rows, self.cols = total.shape[1] // n, total.shape[2] // 2
        low = me % n
        across, along = low % 2, low // 2
        self.spot = (1 - across) * along + across * (n - 1 - along)
        self.peers = [self.index_at((self.spot + step) % n) for step in (1, n - 1)]

    def index_at(self, spot):
        across = spot // (self.n // 2)
        along = (1 - across) * spot + across * (self.n - 1 - spot)
        return self.me - self.me % self.n + 2 * along + across

    def piece(self, chain, step):
        shift = self.n * 4 - step if chain == 0 else step
        return pl.ds(pl.multiple_of((self.spot + shift) % self.n * self.rows, 16), self.rows)

    def half(self, sub):
        return span(sub, self.cols)

    def scatter(self, chain, sub, step):
        return pltpu.make_async_remote_copy(
            self.give.at[chain, sub],
            self.take.at[chain, sub, step],
            self.scatter_sems.at[0, chain, sub, step],
            self.scatter_sems.at[1, chain, sub, step],
            device_id={"dp": self.peers[chain]},
            device_id_type=MESH,
        )

    def gather(self, chain, sub, step):
        part = self.result.at[chain, self.piece(chain, step + self.n - 1), self.half(sub)]
        return pltpu.make_async_remote_copy(
            part,
            part,
            self.gather_sems.at[0, chain, sub, step],
            self.gather_sems.at[1, chain, sub, step],
            device_id={"dp": self.peers[chain]},
            device_id_type=MESH,
        )

    def begin(self, step, chain):
        for sub in range(2):
            self.give[chain, sub] = self.total[chain, self.piece(chain, step), self.half(sub)].astype(BF16)
            self.scatter(chain, sub, step).start()

    def arrived(self, step, chain, sub):
        self.scatter(chain, sub, step).wait()
        mine = self.total[chain, self.piece(chain, step + 1), self.half(sub)]
        return mine + self.take[chain, sub, step].astype(F32)

    def keep(self, step):
        for chain in range(2):
            for sub in range(2):
                value = self.arrived(step, chain, sub)
                self.total[chain, self.piece(chain, step + 1), self.half(sub)] = value

    def pass_on(self, step, sub):
        for chain in range(2):
            self.give[chain, sub] = self.arrived(step, chain, sub).astype(BF16)
            self.scatter(chain, sub, step + 1).start()

    def turn(self, step, sub):
        for chain in range(2):
            value = self.arrived(step, chain, sub).astype(BF16)
            self.give[chain, sub] = value
        for stage in range((self.size // self.n).bit_length() - 1):
            copies = []
            for chain in range(2):
                peer = self.me // self.n
                mine = (peer // (1 << stage)) % 2
                copies.append(
                    pltpu.make_async_remote_copy(
                        self.give.at[chain, sub],
                        self.take.at[chain, sub, self.n - 1 + stage],
                        self.scatter_sems.at[0, chain, sub, self.n - 1 + stage],
                        self.scatter_sems.at[1, chain, sub, self.n - 1 + stage],
                        device_id={"dp": self.me + (1 - 2 * mine) * (self.n << stage)},
                        device_id_type=MESH,
                    )
                )
                copies[-1].start()
            for chain in range(2):
                copies[chain].wait()
                value = self.give[chain, sub].astype(F32) + self.take[chain, sub, self.n - 1 + stage].astype(F32)
                self.give[chain, sub] = value.astype(BF16)
        for chain in range(2):
            self.result[chain, self.piece(chain, self.n - 1), self.half(sub)] = self.give[chain, sub]
            self.gather(chain, sub, 0).start()

    def event(self, number):
        step, sub, n = number // 2, number % 2, self.n

        @pl.when(step < n - 2)
        def _():
            self.pass_on(step, sub)

        @pl.when(step == n - 2)
        def _():
            self.turn(n - 2, sub)

        @pl.when(step >= n - 1)
        def _():
            for chain in range(2):
                self.gather(chain, sub, step - (n - 1)).wait()

            @pl.when(step < 2 * n - 3)
            def _():
                for chain in range(2):
                    self.gather(chain, sub, step - (n - 2)).start()


def ring_scratch(size, rows, cols, steps):
    piece = (rows // min(RING_PIECES, size), cols // 2)
    return [
        pltpu.VMEM((2, 2) + piece, BF16),
        pltpu.VMEM((2, 2, steps) + piece, BF16),
        pltpu.SemaphoreType.DMA((2, 2, 2, steps)),
    ]


X_FAR, X_NEAR, X_LAST, W_IN, W_DOWN, W_OUT, ATT = range(7)
BRANCH, NORMED, OUT, DOUT, DNORMED, DH, DH_NEAR, DH_LAST, GRAD_NEAR = range(7, 16)
KINDS = 16


def first_kernel(
    size, lengths, tok_ref, cot_ref, ln_ref, w_ref, wo_ref, win_hbm, wdn_hbm,
    out_ref, dh_ref, slots_ref, norms_ref, total_hbm, x_hbm, q_hbm, k_hbm, v_hbm, q_rows_hbm, att_hbm, cos_hbm, sin_hbm,
    x_ref, win, wdn, wo_near_ref, att, near, outbox, inbox, low, hat, res, own, r1, dlow, give, take, sums,
    ring_give, ring_take, ring_sems, sems, loads, stores,
):
    rows, width = tok_ref.shape
    hidden = wdn.shape[0] // 2
    cols = wo_ref.shape[0]
    heads = cols // HEAD_DIM
    shards = x_ref.shape[0]
    tokens = shards * rows
    half = width // 2
    chunk = rows // 2
    chunks = [slice(c * chunk, (c + 1) * chunk) for c in range(2)]
    m, me = lax.axis_index("mp"), lax.axis_index("dp")
    core, far = {"mp": peer_of(m, 0)[0]}, {"mp": peer_of(m, 1)[0]}
    ring_peers = Ring(size, me, give, None, None, None, None, None).peers
    greet([core, far] + [{"dp": peer} for peer in ring_peers])

    def post(kind, c, source, target, partner):
        return send(source, target, sems.at[0, kind, c], sems.at[1, kind, c], partner)

    far_copies = [post(X_FAR, c, tok_ref.at[where], x_ref.at[1, where], far) for c, where in enumerate(chunks)]
    near_copy = post(X_NEAR, 0, tok_ref, x_ref.at[2], core)
    weight_copies = [
        post(W_OUT, 0, wo_ref, wo_near_ref, core),
        post(W_IN, 0, win_hbm, win.at[1], core),
        post(W_DOWN, 0, wdn_hbm, wdn.at[pl.ds(hidden, hidden)], core),
    ]
    fetches = []
    for n, (source, target) in enumerate([(win_hbm, win.at[0]), (wdn_hbm, wdn.at[pl.ds(0, hidden)])]):
        fetches.append(pltpu.make_async_copy(source, target, loads.at[n]))
        fetches[-1].start()
    x_ref[0] = tok_ref[...]
    sums[...] = jnp.zeros_like(sums)
    scale_one, shift_one, scale_two, shift_two = (ln_ref[i : i + 1, :] for i in range(4))

    def exchange(kind, value_of):
        copies = []
        for c, where in enumerate(chunks):
            outbox[where, :] = value_of(where).astype(BF16)
            copies.append(post(kind, c, outbox.at[where], inbox.at[where], far))
        return copies

    def branch(index, where):
        return mm(att[index, :, where], wo_ref[...], TN) + mm(near[index, :, where], wo_near_ref[...], TN)

    def attention(q_ref, k_ref, v_ref, k_rows_ref, q_rows_ref, cos_ref, sin_ref, top_ref, acc_ref):
        half_head = HEAD_DIM // 2
        starts, ends, end = [], [], 0
        for d in range(lengths.shape[1]):
            starts.append(end)
            end = end + lengths[0, d]
            ends.append(end)
        doc = lax.broadcasted_iota(jnp.int32, (16, rows), 0)
        first, last = jnp.zeros((16, rows), jnp.int32), jnp.zeros((16, rows), jnp.int32)
        for d in range(lengths.shape[1]):
            first, last = jnp.where(doc == d, starts[d], first), jnp.where(doc == d, ends[d], last)
        exponent = lax.broadcasted_iota(jnp.int32, (half_head, rows), 0).astype(F32)
        rate = jnp.exp(exponent * (-2.0 * math.log(1000.0) / HEAD_DIM))
        row = lax.broadcasted_iota(jnp.int32, (48, rows), 0)
        ones = jnp.where(row < 3, 1.0, 0.0)
        v_tail = jnp.concatenate([ones, jnp.zeros((16, rows), F32)], axis=0)
        top_ref[...] = jnp.full_like(top_ref, FAR)
        acc_ref[...] = jnp.zeros_like(acc_ref)

        def tables(slot):
            where = slice(slot * rows, (slot + 1) * rows)
            shard = 2 * ((slot % 2 + m // 2) % 2) + (slot // 2 + m) % 2
            token = lax.broadcasted_iota(jnp.int32, (16, rows), 1) + shard * rows
            inside = (token >= first) & (token < last)
            begin = jnp.max(jnp.where(inside, first, 0), axis=0, keepdims=True)
            angles = rate * (token[0:1] - begin).astype(F32)
            cos_ref[:, where], sin_ref[:, where] = jnp.cos(angles), jnp.sin(angles)
            for h in range(heads):
                q_ref[h, HEAD_DIM:, where] = jnp.concatenate(
                    [jnp.where(inside, 0.0, FAR), jnp.zeros((48, rows), F32)], axis=0
                ).astype(BF16)
                k_ref[h, HEAD_DIM:, where] = jnp.concatenate([jnp.where(inside, 1.0, 0.0), ones], axis=0).astype(BF16)
                v_ref[h, HEAD_DIM:, where] = v_tail.astype(BF16)

        def project(slot):
            where = slice(slot * rows, (slot + 1) * rows)
            projected = mm(w_ref[...], x_ref[slot], NT)
            cosine, sine = cos_ref[:, where], sin_ref[:, where]

            def rotated(start, scale):
                one, two = projected[start : start + half_head], projected[start + half_head : start + HEAD_DIM]
                turned = jnp.concatenate([one * cosine - two * sine, two * cosine + one * sine], axis=0)
                return turned * scale

            for h in range(heads):
                q_ref[h, :HEAD_DIM, where] = rotated(h * HEAD_DIM, LOG2E / math.sqrt(HEAD_DIM)).astype(BF16)
                k = rotated(cols + h * HEAD_DIM, 1.0)
                k_ref[h, :HEAD_DIM, where] = k.astype(BF16)
                tail = k_ref[h, HEAD_DIM:, where].astype(F32)
                k_rows_ref[h, where, :] = jnp.concatenate([k, tail], axis=0).T.astype(BF16)
                start = 2 * cols + h * HEAD_DIM
                v_ref[h, :HEAD_DIM, where] = projected[start : start + HEAD_DIM].astype(BF16)

        def pairs(count, pair):
            def run(n, carry):
                qs, ks = pair(n)
                queries, keys = span(qs, rows), span(ks, rows)
                for h in range(heads):
                    s = mm(k_rows_ref[h, keys, :], q_ref[h, :, queries])
                    old = top_ref[qs, h, 0:1, :]
                    top = jnp.maximum(old, jnp.max(s, axis=0, keepdims=True))
                    probs = jnp.exp2(s - top).astype(BF16)
                    top_ref[qs, h, 0:1, :] = top
                    acc_ref[qs, h] = acc_ref[qs, h] * jnp.exp2(old - top) + mm(v_ref[h, :80, keys], probs)
                return carry

            lax.fori_loop(0, count, run, 0)

        writes = []

        def write(source, target):
            writes.append(pltpu.make_async_copy(source, target, stores.at[len(writes)]))
            writes[-1].start()

        def settle(slot):
            where = slice(slot * rows, (slot + 1) * rows)
            for h in range(heads):
                total = acc_ref[slot, h, HEAD_DIM : HEAD_DIM + 1, :]
                out = acc_ref[slot, h, :HEAD_DIM, :] / total
                att[slot, h * HEAD_DIM : (h + 1) * HEAD_DIM, :] = out.astype(BF16)
                level = top_ref[slot, h, 0:1, :] + jnp.log2(total)
                query = q_ref[h, :, where].astype(F32)
                wide = jnp.concatenate([query[:80], thirds(-level), query[96:]], axis=0)
                q_rows_ref[h, where, :] = wide.T.astype(BF16)

        for slot in range(4):
            tables(slot)
        project(0)
        near_copy.wait()
        project(2)
        pairs(4, lambda n: (2 * (n // 2), 2 * (n % 2)))
        last_copies = []
        for c, where in enumerate(chunks):
            far_copies[c].wait()
            last_copies.append(post(X_LAST, c, x_ref.at[1, where], x_ref.at[3, where], core))
        project(1)
        for copy in last_copies:
            copy.wait()
        project(3)
        for source, target in [
            (x_ref, x_hbm), (q_ref, q_hbm), (k_ref, k_hbm), (v_ref, v_hbm), (cos_ref, cos_hbm), (sin_ref, sin_hbm)
        ]:
            write(source, target)
        pairs(4, lambda n: (3, n))
        settle(3)
        copies = [post(ATT, 1, att.at[3], near.at[1], core)]
        pairs(4, lambda n: (1, n))
        settle(1)
        weight_copies[0].wait()
        copies[0].wait()
        exchange(BRANCH, lambda where: branch(1, where))
        pairs(4, lambda n: (2 * (1 - n // 2), 2 * (n % 2) + 1))
        settle(2)
        copies.append(post(ATT, 0, att.at[2], near.at[0], core))
        settle(0)
        write(q_rows_ref, q_rows_hbm)
        write(att, att_hbm)
        copies[1].wait()
        for where in chunks:
            hat[where, :] = tok_ref[where, :].astype(F32) + branch(0, where)
        for copy in writes:
            copy.wait()

    along = pltpu.VMEM((heads, LANES, tokens), BF16)
    down = pltpu.VMEM((heads, tokens, LANES), BF16)
    table = pltpu.VMEM((HEAD_DIM // 2, tokens), F32)
    pl.run_scoped(
        attention, along, along, along, down, down, table, table,
        pltpu.VMEM((shards, heads, 8, rows), F32), pltpu.VMEM((shards, heads, 80, rows), F32),
    )
    branch_copies = [
        pltpu.make_async_remote_copy(
            outbox.at[where],
            inbox.at[where],
            sems.at[0, BRANCH, c],
            sems.at[1, BRANCH, c],
            device_id=far,
            device_id_type=MESH,
        )
        for c, where in enumerate(chunks)
    ]

    def by_parts(c, part):
        step = 64

        def run(i, carry):
            part(pl.ds(pl.multiple_of(c * chunk + i * step, step), step))
            return carry

        lax.fori_loop(0, chunk // step, run, 0)

    def mean(values):
        return jnp.sum(values, axis=-1, keepdims=True) * (1.0 / width)

    def add_up(index, values):
        sums[index] += jnp.sum(values.reshape(values.shape[0] // 8, 8, width), axis=0)

    def norm_one(where):
        h = hat[where, :] + inbox[where, :].astype(F32)
        h = h - mean(h)
        r = lax.rsqrt(mean(h * h) + EPSILON)
        h = h * r
        hat[where, :] = h
        r1[where, :] = jnp.broadcast_to(r, (r.shape[0], LANES))
        h = h * scale_one + shift_one
        res[where, :] = h
        low[0, where, :] = h.astype(BF16)

    normed_copies = []
    for c, where in enumerate(chunks):
        branch_copies[c].wait()
        by_parts(c, norm_one)
        normed_copies.append(post(NORMED, c, low.at[0, where], low.at[1, where], far))
    for copy in fetches + weight_copies[1:]:
        copy.wait()

    def feed_forward(gu, hid, total):
        ring = Ring(size, me, total, ring_give, ring_take, None, ring_sems, None)
        tile = hidden // 2

        def mlp(side, where):
            def columns(t, carry):
                k, at = t // 2, (t % 2) * tile
                x = low[side, where, :]
                gate_at = pl.ds(pl.multiple_of(at, LANES), tile)
                up_at = pl.ds(pl.multiple_of(hidden + at, LANES), tile)
                gate, up = mm(x, win[k, :, gate_at]), mm(x, win[k, :, up_at])
                gu[side, k, where, gate_at] = gate.astype(BF16)
                gu[side, k, where, up_at] = up.astype(BF16)
                value = gate * jax.nn.sigmoid(gate) * up
                hid[side, where, pl.ds(pl.multiple_of(k * hidden + at, LANES), tile)] = value.astype(BF16)
                return carry

            lax.fori_loop(0, 4, columns, 0)
            return mm(hid[side, where, :], wdn[...])

        def both_sides(copies_in, kind, compute):
            copies = []
            for c, where in enumerate(chunks):
                own[where, :] = compute(0, where)
                copies_in[c].wait()
                outbox[where, :] = compute(1, where).astype(BF16)
                copies.append(post(kind, c, outbox.at[where], inbox.at[where], far))
            return copies

        out_copies = both_sides(normed_copies, OUT, mlp)

        def norm_two(where):
            z = res[where, :] + own[where, :] + inbox[where, :].astype(F32)
            z = z - mean(z)
            r = lax.rsqrt(mean(z * z) + EPSILON)
            z = z * r
            out_ref[where, :] = (z * scale_two + shift_two).astype(BF16)
            g = cot_ref[where, :].astype(F32)
            add_up(2, g * z)
            add_up(3, g)
            e = g * scale_two
            dz = r * (e - mean(e) - z * mean(e * z))
            res[where, :] = dz
            dlow[0, where, :] = dz.astype(BF16)

        dout_copies = []
        for c, where in enumerate(chunks):
            out_copies[c].wait()
            by_parts(c, norm_two)
            dout_copies.append(post(DOUT, c, dlow.at[0, where], dlow.at[1, where], far))

        def mlp_back(side, where):
            def columns(t, carry):
                k, at = t // 2, (t % 2) * tile
                d_hidden = mm(
                    dlow[side, where, :], wdn[pl.ds(pl.multiple_of(k * hidden + at, LANES), tile), :], NT
                )
                gate_at = pl.ds(pl.multiple_of(at, LANES), tile)
                up_at = pl.ds(pl.multiple_of(hidden + at, LANES), tile)
                gate, up = gu[side, k, where, gate_at].astype(F32), gu[side, k, where, up_at].astype(F32)
                s = jax.nn.sigmoid(gate)
                gu[side, k, where, gate_at] = (d_hidden * up * s * (1.0 + gate * (1.0 - s))).astype(BF16)
                gu[side, k, where, up_at] = (d_hidden * gate * s).astype(BF16)
                return carry

            lax.fori_loop(0, 4, columns, 0)
            return mm(gu[side, 0, where, :], win[0], NT) + mm(gu[side, 1, where, :], win[1], NT)

        dnormed_copies = both_sides(dout_copies, DNORMED, mlp_back)

        def weight_grads(k, target, then=lambda r: None):
            def chain(r, carry):
                at = pl.ds(pl.multiple_of(r * half, LANES), half)
                for n, place in enumerate((slice(0, hidden), slice(hidden, 2 * hidden))):
                    piece = mm(low[0, :, at], gu[0, k, :, place], TN) + mm(low[1, :, at], gu[1, k, :, place], TN)
                    target[r, n * half : (n + 1) * half, :] = piece.astype(target.dtype)
                at = pl.ds(pl.multiple_of(k * hidden + r * half, LANES), half)
                piece = mm(hid[0, :, at], dlow[0], TN) + mm(hid[1, :, at], dlow[1], TN)
                target[r, 2 * half : 3 * half, :] = piece.astype(target.dtype)
                then(r)
                return carry

            lax.fori_loop(0, 2, chain, 0)

        def grad_copy(r):
            return pltpu.make_async_remote_copy(
                give.at[r],
                take.at[r],
                sems.at[0, GRAD_NEAR, r],
                sems.at[1, GRAD_NEAR, r],
                device_id=core,
                device_id_type=MESH,
            )

        weight_grads(1, give, lambda r: grad_copy(r).start())

        def norm_one_back(where):
            d = res[where, :] + own[where, :] + inbox[where, :].astype(F32)
            h = hat[where, :]
            add_up(0, d * h)
            add_up(1, d)
            e = d * scale_one
            dh = r1[where, 0:1] * (e - mean(e) - h * mean(e * h))
            dh_ref[where, :] = dh
            slots_ref[0, where, :] = dh.astype(BF16)

        dh_copies, last_copies = [], []

        def dh_chunk(c):
            where = chunks[c]
            dnormed_copies[c].wait()
            by_parts(c, norm_one_back)
            mine = slots_ref.at[0, where]
            dh_copies.append(post(DH, c, mine, slots_ref.at[1, where], far))
            last_copies.append(post(DH_NEAR, c, mine, slots_ref.at[2, where], core))

        dh_chunk(0)
        weight_grads(0, total)
        dh_chunk(1)
        for r in range(2):
            grad_copy(r).wait()
            total[r] += take[r].astype(F32)
            ring.begin(0, r)

        def hand_on(c):
            dh_copies[c].wait()
            where = chunks[c]
            last_copies.append(post(DH_LAST, c, slots_ref.at[1, where], slots_ref.at[3, where], core))

        for i in range(4):
            norms_ref[i : i + 1, :] = jnp.sum(sums[i], axis=0, keepdims=True)
        norms_ref[4:8, :] = jnp.zeros((4, width), F32)
        hand_on(0)
        for step in range(RING_EARLY - 1):
            for sub in range(2):
                ring.pass_on(step, sub)
        hand_on(1)
        ring.keep(RING_EARLY - 1)
        write = pltpu.make_async_copy(total, total_hbm, loads.at[0])
        write.start()
        for copy in last_copies:
            copy.wait()
        write.wait()

    pl.run_scoped(
        feed_forward,
        pltpu.VMEM((2, 2, rows, 2 * hidden), BF16),
        pltpu.VMEM((2, rows, 2 * hidden), BF16),
        pltpu.VMEM((2, 3 * half, width), F32),
    )


def first(lengths, tokens, cotangent, norms, w_turned, w_out, w_in, w_down):
    size, shards = lax.axis_size("dp"), lax.axis_size("mp")
    rows, width = tokens.shape
    cols, hidden = w_out.shape[0], w_down.shape[0]
    heads, length = cols // HEAD_DIM, rows * shards
    chain = 3 * width // 2
    vmem = pl.BlockSpec(memory_space=pltpu.VMEM)
    hbm = pl.BlockSpec(memory_space=pl.ANY)
    dma = pltpu.SemaphoreType.DMA
    shape = jax.ShapeDtypeStruct
    along, table = shape((heads, LANES, length), BF16), shape((HEAD_DIM // 2, length), F32)
    wide = lambda dtype, *lead: pltpu.VMEM(lead + (rows, width), dtype)
    return pl.pallas_call(
        functools.partial(first_kernel, size),
        out_shape=(
            shape((rows, width), BF16),
            shape((rows, width), F32),
            shape((shards, rows, width), BF16),
            shape((8, width), F32),
            shape((2, chain, width), F32),
            shape((shards, rows, width), BF16),
            along,
            along,
            along,
            shape((heads, length, LANES), BF16),
            shape((shards, cols, rows), BF16),
            table,
            table,
        ),
        in_specs=[pl.BlockSpec(memory_space=pltpu.SMEM)] + [vmem] * 5 + [hbm] * 2,
        out_specs=[vmem] * 4 + [hbm] * 9,
        scratch_shapes=[
            wide(BF16, shards),
            pltpu.VMEM((2, width, 2 * hidden), BF16),
            pltpu.VMEM((2 * hidden, width), BF16),
            pltpu.VMEM((cols, width), BF16),
            pltpu.VMEM((shards, cols, rows), BF16),
            pltpu.VMEM((2, cols, rows), BF16),
            wide(BF16),
            wide(BF16),
            wide(BF16, 2),
            wide(F32),
            wide(F32),
            wide(F32),
            pltpu.VMEM((rows, LANES), F32),
            wide(BF16, 2),
            pltpu.VMEM((2, chain, width), BF16),
            pltpu.VMEM((2, chain, width), BF16),
            pltpu.VMEM((4, 8, width), F32),
            *ring_scratch(size, chain, width, RING_EARLY),
            dma((2, KINDS, 2)),
            dma((2,)),
            dma((8,)),
        ],
        compiler_params=pltpu.CompilerParams(
            collective_id=0, has_side_effects=True, vmem_limit_bytes=WIDE_LIMIT
        ),
        cost_estimate=pl.CostEstimate(
            flops=36 * rows * width * hidden, bytes_accessed=40 * rows * width, transcendentals=0
        ),
        name="first",
    )(lengths, tokens, cotangent, norms, w_turned, w_out, w_in, w_down)


class Sum:
    def __init__(self, size, me, first, total, give, take, result, sems):
        orders = dp_orders(size)
        self.total, self.give, self.take, self.result, self.sems = total, give, take, result, sems
        halving, stages = halvings(size), size.bit_length() - 1
        count = 1 << (halving - first)
        self.rows = total.shape[1] // count
        base, low, peers = [], [0, 0], []
        for chain in range(2):
            peers.append([peer_of(me, bit) for bit in orders[chain]])
            base.append(sum(peers[chain][done][1] * (1 << (halving - 1 - done)) for done in range(first)))
        self.steps, spot = [], 0
        for stage in range(first, stages):
            halve = stage < halving
            part = count // 2 if halve else count
            step = dict(kind="halve" if halve else "swap", part=part, spot=spot, chains=[], last=stage + 1 == stages)
            for chain in range(2):
                peer, mine = peers[chain][stage]
                away = low[chain] + (1 - mine) * part if halve else low[chain]
                low[chain] = low[chain] + mine * part if halve else low[chain]
                step["chains"].append(dict(peer=peer, away=away, keep=low[chain], final=base[chain] + low[chain]))
            self.steps.append(step)
            spot, count = spot + part, part
        low = [base[chain] + low[chain] for chain in range(2)]
        for stage in reversed(range(halving)):
            step = dict(kind="gather", part=count, chains=[])
            for chain in range(2):
                peer, mine = peers[chain][stage]
                step["chains"].append(dict(peer=peer, away=low[chain]))
                low[chain] = low[chain] - mine * count
            self.steps.append(step)
            count *= 2

    def block(self, low, count):
        return pl.ds(pl.multiple_of(low * self.rows, 16), count * self.rows)

    def copy(self, index, chain):
        step = self.steps[index]
        one = step["chains"][chain]
        if step["kind"] == "gather":
            source = target = self.result.at[chain, self.block(one["away"], step["part"])]
        else:
            spot = pl.ds(step["spot"] * self.rows, step["part"] * self.rows)
            source, target = self.give.at[chain, spot], self.take.at[chain, spot]
        return pltpu.make_async_remote_copy(
            source,
            target,
            self.sems.at[0, chain, index],
            self.sems.at[1, chain, index],
            device_id={"dp": one["peer"]},
            device_id_type=MESH,
        )

    def start(self, index):
        step = self.steps[index]
        for chain in range(2):
            if step["kind"] != "gather":
                spot = pl.ds(step["spot"] * self.rows, step["part"] * self.rows)
                away = self.block(step["chains"][chain]["away"], step["part"])
                self.give[chain, spot, :] = self.total[chain, away, :].astype(BF16)
            self.copy(index, chain).start()

    def finish(self, index):
        step = self.steps[index]
        for chain in range(2):
            self.copy(index, chain).wait()
            if step["kind"] == "gather":
                continue
            one = step["chains"][chain]
            spot = pl.ds(step["spot"] * self.rows, step["part"] * self.rows)
            keep = self.block(one["keep"], step["part"])
            mine = self.total[chain, keep, :] if step["kind"] == "halve" else self.give[chain, spot, :].astype(F32)
            value = mine + self.take[chain, spot, :].astype(F32)
            if step["last"]:
                self.result[chain, self.block(one["final"], 1), :] = value.astype(BF16)
            else:
                self.total[chain, keep, :] = value

    def advance(self, index):
        self.finish(index)
        if index + 1 < len(self.steps):
            self.start(index + 1)


def pieces_sent(size, first):
    halving = halvings(size)
    return (1 << (halving - first)) - 1 + size.bit_length() - 1 - halving


def back_kernel(
    size, att_ref, w_out_ref, cos_ref, sin_ref, norms_ref, w_ref, w_near_ref, dh_ref,
    total_hbm, slots_hbm, q_rows_hbm, q_hbm, k_hbm, v_hbm, x_hbm,
    dx_ref, grad_ref, big_ref, sums_ref,
    big, slots, q_rows_ref, q_ref, k_ref, v_ref, x_ref,
    do_ref, do_rows_ref, dq_ref, dk_ref, dv_ref, d_qkv,
    total, give, take, near, far_out, far_in, own, norm_in,
    ring_give, ring_take, ring_sems, gather_sems, loads, near_sem, far_sem, sum_sems, norm_sem,
):
    heads, _, tokens = k_ref.shape
    shards, rows, width = slots.shape
    cols = heads * HEAD_DIM
    half = HEAD_DIM // 2
    m, me = lax.axis_index("mp"), lax.axis_index("dp")
    stages = size.bit_length() - 1
    core, far = {"mp": peer_of(m, 0)[0]}, {"mp": peer_of(m, 1)[0]}
    partners = [core, far] + [{"dp": peer_of(me, bit)[0]} for bit in range(stages)]
    sources = [total_hbm, slots_hbm, q_rows_hbm, q_hbm, k_hbm, v_hbm, x_hbm]
    targets = [big, slots, q_rows_ref, q_ref, k_ref, v_ref, x_ref]
    fetches = [
        pltpu.make_async_copy(source, target, loads.at[n])
        for n, (source, target) in enumerate(zip(sources, targets))
    ]
    for fetch in fetches:
        fetch.start()
    ring = Ring(size, me, big, ring_give, ring_take, big_ref, ring_sems, gather_sems)
    greet(partners + [{"dp": peer} for peer in ring.peers])
    sums_ref[...] = norms_ref[...]
    small = Sum(size, me, 0, total, give, take, grad_ref, sum_sems)
    fetches[0].wait()
    for chain in range(2):
        ring.begin(RING_EARLY, chain)
    fetches[1].wait()
    events = 2 * (2 * ring.n - 2)
    first_event = 2 * RING_EARLY

    def prepare(i, carry):
        d_att = mm(w_out_ref[...], slots[i], NT).astype(BF16)
        do_ref[:, span(i, rows)] = d_att
        products = d_att.astype(F32) * att_ref[i].astype(F32)
        for h in range(heads):
            mine = slice(h * HEAD_DIM, (h + 1) * HEAD_DIM)
            dot = jnp.sum(products[mine], axis=0, keepdims=True)
            wide = [d_att[mine].astype(F32), thirds(-dot), jnp.zeros((LANES - HEAD_DIM - 16, rows), F32)]
            do_rows_ref[h, span(i, rows), :] = jnp.concatenate(wide, axis=0).T.astype(BF16)
        return carry

    lax.fori_loop(0, shards, prepare, 0)
    dq_ref[...] = jnp.zeros_like(dq_ref)
    for fetch in fetches[2:]:
        fetch.wait()

    def rotated_back(values, cosine, sine):
        first, second = values[:half], values[half:]
        return [first * cosine + second * sine, second * cosine - first * sine]

    def over_keys(j, carry):
        keys = span(j, rows)
        dk_ref[...] = jnp.zeros_like(dk_ref)
        dv_ref[...] = jnp.zeros_like(dv_ref)

        def over_queries(i, carry):
            queries = span(i, rows)
            for h in range(heads):
                k = k_ref[h, :, keys]
                probs = jnp.exp2(mm(q_rows_ref[h, queries, :], k))
                d_scores = (probs * mm(do_rows_ref[h, queries, :], v_ref[h, :, keys])).astype(BF16)
                dv_ref[h] += mm(do_ref[h * HEAD_DIM : (h + 1) * HEAD_DIM, queries], probs.astype(BF16))
                dk_ref[h] += mm(q_ref[h, :HEAD_DIM, queries], d_scores)
                dq_ref[h, :, queries] += mm(k[:HEAD_DIM], d_scores, NT)
            number = first_event + j * shards + i
            pl.when(number < events)(lambda: ring.event(number))
            return carry

        lax.fori_loop(0, shards, over_queries, 0)
        cosine, sine = cos_ref[:, keys] * (1.0 / LOG2E), sin_ref[:, keys] * (1.0 / LOG2E)
        pieces = []
        for h in range(heads):
            pieces += rotated_back(dk_ref[h], cosine, sine)
        pieces += [dv_ref[h] for h in range(heads)]
        d_qkv[j, cols:, :] = jnp.concatenate(pieces, axis=0).astype(BF16)
        return carry

    lax.fori_loop(0, shards, over_keys, 0)
    first_event = min(first_event + shards * shards, events)
    for i in range(shards):
        scale = 1.0 / math.sqrt(HEAD_DIM)
        cosine, sine = cos_ref[:, span(i, rows)] * scale, sin_ref[:, span(i, rows)] * scale
        pieces = []
        for h in range(heads):
            pieces += rotated_back(dq_ref[h, :, span(i, rows)], cosine, sine)
        d_qkv[i, :cols, :] = jnp.concatenate(pieces, axis=0).astype(BF16)
    near_copy = send(d_qkv.at[pl.ds(2, 2)], near, near_sem.at[0], near_sem.at[1], core)

    def product(first, count):
        piece = mm(d_qkv[0, first : first + count, :], x_ref[0])
        for slot in range(1, shards):
            piece += mm(d_qkv[slot, first : first + count, :], x_ref[slot])
        return piece

    chain_rows = total.shape[1]
    total[0] = product(0, chain_rows)
    total[1, :cols, :] = product(chain_rows, cols)
    piece = mm(att_ref[0], slots[0])
    for slot in range(1, shards):
        piece += mm(att_ref[slot], slots[slot])
    total[1, cols:, :] = piece
    small.start(0)

    def norm_exchange(stage):
        return send(sums_ref, norm_in.at[stage], norm_sem.at[0, stage], norm_sem.at[1, stage], partners[stage])

    norm_copy, norm_done = norm_exchange(0), 0
    near_copy.wait()

    def d_tokens(index):
        return mm(d_qkv[index], w_ref[...], TN) + mm(near[index], w_near_ref[...], TN)

    far_out[...] = d_tokens(1).astype(BF16)
    far_copy = send(far_out, far_in, far_sem.at[0], far_sem.at[1], far)
    own[...] = dh_ref[...] + d_tokens(0)

    left, share = first_event, -(-(events - first_event) // len(small.steps))
    small_done = 0
    while small_done < len(small.steps) or norm_done < len(partners):
        if small_done < len(small.steps):
            small.advance(small_done)
            small_done += 1
            for number in range(left, min(left + share, events)):
                ring.event(number)
            left = min(left + share, events)
        if norm_done < len(partners):
            norm_copy.wait()
            sums_ref[...] += norm_in[norm_done]
            norm_done += 1
            if norm_done < len(partners):
                norm_copy = norm_exchange(norm_done)
    far_copy.wait()
    dx_ref[...] = (own[...] + far_in[...].astype(F32)).astype(BF16)


def back(att, w_out, cosine, sine, norms, w_turned, w_near, dh, totals, dh_slots, q_rows, q, k, v, x_slots):
    size = lax.axis_size("dp")
    stages = size.bit_length() - 1
    heads, _, tokens = q.shape
    shards, rows, width = x_slots.shape
    cols = w_turned.shape[0]
    chain, big_chain = width // 2, totals.shape[1]
    sent = pieces_sent(size, 0) * (chain >> halvings(size))
    spots = min(RING_PIECES, size)
    ring_steps = spots - 1 + (size // spots).bit_length() - 1
    steps = stages + halvings(size)
    vmem = pl.BlockSpec(memory_space=pltpu.VMEM)
    hbm = pl.BlockSpec(memory_space=pl.ANY)
    dma = pltpu.SemaphoreType.DMA
    along = pltpu.VMEM((heads, LANES, tokens), BF16)
    return pl.pallas_call(
        functools.partial(back_kernel, size),
        out_shape=(
            jax.ShapeDtypeStruct((rows, width), BF16),
            jax.ShapeDtypeStruct((2, chain, width), BF16),
            jax.ShapeDtypeStruct((2, big_chain, width), BF16),
            jax.ShapeDtypeStruct(norms.shape, F32),
        ),
        in_specs=[vmem] * 8 + [hbm] * 7,
        out_specs=[vmem] * 4,
        scratch_shapes=[
            pltpu.VMEM(totals.shape, F32),
            pltpu.VMEM(dh_slots.shape, BF16),
            pltpu.VMEM((heads, tokens, LANES), BF16),
            along,
            along,
            along,
            pltpu.VMEM(x_slots.shape, BF16),
            pltpu.VMEM((heads * HEAD_DIM, tokens), BF16),
            pltpu.VMEM((heads, tokens, LANES), BF16),
            pltpu.VMEM((heads, HEAD_DIM, tokens), F32),
            pltpu.VMEM((heads, HEAD_DIM, rows), F32),
            pltpu.VMEM((heads, HEAD_DIM, rows), F32),
            pltpu.VMEM((shards, cols, rows), BF16),
            pltpu.VMEM((2, chain, width), F32),
            pltpu.VMEM((2, sent, width), BF16),
            pltpu.VMEM((2, sent, width), BF16),
            pltpu.VMEM((2, cols, rows), BF16),
            pltpu.VMEM((rows, width), BF16),
            pltpu.VMEM((rows, width), BF16),
            pltpu.VMEM((rows, width), F32),
            pltpu.VMEM((2 + stages,) + norms.shape, F32),
            *ring_scratch(size, big_chain, width, ring_steps),
            dma((2, 2, 2, spots - 1)),
            dma((7,)),
            dma((2,)),
            dma((2,)),
            dma((2, 2, steps)),
            dma((2, 2 + stages)),
        ],
        compiler_params=pltpu.CompilerParams(
            collective_id=1, has_side_effects=True, vmem_limit_bytes=WIDE_LIMIT
        ),
        cost_estimate=pl.CostEstimate(
            flops=5 * heads * tokens * tokens * LANES, bytes_accessed=60 * rows * width, transcendentals=0
        ),
        name="back",
    )(att, w_out, cosine, sine, norms, w_turned, w_near, dh, totals, dh_slots, q_rows, q, k, v, x_slots)


def emit_kernel(big_ref, small_ref, gate_up_ref, down_ref, qkv_ref, out_ref):
    for n in range(2):
        gate_up_ref[:, n, :] = big_ref[0, n].astype(F32)
    down_ref[...] = big_ref[0, 2].astype(F32)
    qkv_steps = pl.num_programs(0) * 3 // 4

    @pl.when(pl.program_id(0) < qkv_steps)
    def _():
        qkv_ref[...] = small_ref[0].astype(F32)

    @pl.when(pl.program_id(0) >= qkv_steps)
    def _():
        out_ref[...] = small_ref[0].astype(F32)


def emit(big, small):
    _, chain, width = small.shape
    steps = 8
    per, rows = steps // 2, width // steps
    qkv_steps = steps * 3 // 4
    shape = lambda *dims: jax.ShapeDtypeStruct(dims, F32)
    return pl.pallas_call(
        emit_kernel,
        out_shape=(
            shape(width, 2, width),
            shape(width, width),
            shape(qkv_steps * rows, width),
            shape((steps - qkv_steps) * rows, width),
        ),
        grid=(steps,),
        in_specs=[
            pl.BlockSpec((1, 3, rows, width), lambda i: (i // per, 0, i % per, 0)),
            pl.BlockSpec((1, rows, width), lambda i: (i // per, i % per, 0)),
        ],
        out_specs=[
            pl.BlockSpec((rows, 2, width), lambda i: (i, 0, 0)),
            pl.BlockSpec((rows, width), lambda i: (i, 0)),
            pl.BlockSpec((rows, width), lambda i: (jnp.minimum(i, qkv_steps - 1), 0)),
            pl.BlockSpec((rows, width), lambda i: (jnp.maximum(i - qkv_steps, 0), 0)),
        ],
        compiler_params=pltpu.CompilerParams(vmem_limit_bytes=VMEM_LIMIT),
        cost_estimate=pl.CostEstimate(flops=0, bytes_accessed=24 * width * width, transcendentals=0),
        name="emit",
    )(big.reshape(2, 3, chain, width), small)


def body(
    tokens, lengths, w_qkv, w_out, w_gate_up, w_down, ln1_scale, ln1_shift, ln2_scale, ln2_shift, cotangent
):
    rows, width = tokens.shape
    shards = lax.axis_size("mp")
    local_cols = w_out.shape[0]
    hidden_cols = w_down.shape[0]
    m = lax.axis_index("mp")
    qkv_turned = w_qkv.transpose(1, 2, 0).reshape(3 * local_cols, width)
    qkv_near = lax.ppermute(qkv_turned, "mp", [(i, i ^ 1) for i in range(shards)])
    norms = jnp.concatenate([jnp.stack([ln1_scale, ln1_shift, ln2_scale, ln2_shift]), jnp.zeros((4, width), F32)])
    output, dh, dh_slots, norms, totals, x_slots, q, k, v, q_rows, att, cosine, sine = first(
        lengths, tokens, cotangent, norms, qkv_turned, w_out, w_gate_up.reshape(width, 2 * hidden_cols), w_down
    )
    d_tokens, small, big, norms = back(
        att, w_out, cosine, sine, norms, qkv_turned, qkv_near, dh, totals, dh_slots, q_rows, q, k, v, x_slots
    )
    grad_gate_up, grad_down, grad_qkv, grad_out = emit(big, small)
    grad_qkv = grad_qkv.reshape(3, local_cols, width).transpose(2, 0, 1)
    norms = lax.dynamic_slice_in_dim(norms, m * local_cols, local_cols, 1)
    return (
        output,
        d_tokens,
        grad_qkv,
        grad_out,
        grad_gate_up,
        grad_down,
        norms[0],
        norms[1],
        norms[2],
        norms[3],
    )


def solution(mesh):
    return jax.shard_map(
        body,
        mesh=mesh,
        in_specs=(
            P(("dp", "mp"), None),
            P("dp", None),
            P(None, None, "mp"),
            P("mp", None),
            P(None, None, "mp"),
            P("mp", None),
            P(),
            P(),
            P(),
            P(),
            P(("dp", "mp"), None),
        ),
        out_specs=(
            P(("dp", "mp"), None),
            P(("dp", "mp"), None),
            P(None, None, "mp"),
            P("mp", None),
            P(None, None, "mp"),
            P("mp", None),
            P("mp"),
            P("mp"),
            P("mp"),
            P("mp"),
        ),
        check_vma=False,
    )
```

time: 308 us -> 268 us (0.87)
  Pallas kernels: 276 us -> 255 us
  waiting for transfers between devices: 11.9 us -> 0.01 us
  other arithmetic: 6.54 us -> 0 us
  local copies, waits for them, and re-layouts: 6.83 us -> 11.1 us
  starting transfers between devices: 4.62 us -> 0.52 us
    pallas_call x1, Pallas kernels: 117 us -> 98.4 us  [back(): pl.pallas_call(functools.partial(back_kernel, size), out_shape=(jax.Shape...]
    ppermute x7 -> x1, waiting for transfers between devices: 11.9 us -> 0.01 us  [body(): lax.ppermute(qkv_turned, 'mp', [(i, i ^ 1) for i in range(shards)])]
    ppermute x7 -> x1, starting transfers between devices: 4.62 us -> 0.52 us  [body(): lax.ppermute(qkv_turned, 'mp', [(i, i ^ 1) for i in range(shards)])]
    another operation x3 -> x0, other arithmetic: 3.69 us -> none  [the longest x1 2.97 us: body(): x_slots = jnp.stack([tokens, x_far, x_near, x_last])]
    pallas_call x3 -> x1, Pallas kernels: 151 us -> 148 us  [first(): pl.pallas_call(functools.partial(first_kernel, size), out_shape=(shape((r...]
    unnamed x23 -> x9, local copies, waits for them, and re-layouts: 3.98 us -> 6.17 us
  transfers between devices with their start and end apart: 7 -> 1, of which waited for: 1 -> 0; matrix products, arithmetic and copies ran while one was open for 3% -> 3% of each run, Pallas kernels for 49% -> 55%
where the time goes in v1:
time: 268 us; the launch traced here: 267 us
  Pallas kernels  255 us (95%)
  local copies, waits for them, and re-layouts  11.1 us (4%)
    pallas_call x1, Pallas kernels, first(): pl.pallas_call(functools.partial(first_kernel, size), out_shape=(shape((r...  148 us
    pallas_call x1, Pallas kernels, back(): pl.pallas_call(functools.partial(back_kernel, size), out_shape=(jax.Shape...  98.4 us
    pallas_call x1, Pallas kernels, emit(): pl.pallas_call(emit_kernel, out_shape=(shape(width, 2, width), shape(widt...  8.3 us
    unnamed x9, local copies, waits for them, and re-layouts  6.17 us
  transfers between devices with their start and end apart: 1, of which 0 were waited for; matrix products, arithmetic and copies ran while one was open for 3% of the time, Pallas kernels for 55%

profile of v1, /device:TPU:0, one launch (start us, length us, event | category | flops | bytes accessed | tf_op | source)
XLA Modules:
  0.0 267.3 jit_solution(14455120810226002475)
XLA Ops:
  0.6 0.5 collective-permute-start
  1.2 0.7 stack.12
  1.8 0.7 stack.13
  2.5 0.7 stack.14
  3.2 0.7 stack.15
  3.9 3.5 %copy.21 = bf16[96,8,2,768]{3,1,2,0:T(8,128)(2,1)} copy(bf16[96,8,2,768]{3,2,1,0:T(2,128)(2,1)} %bitcast.14) | data formatting | bytes 4718592
  7.4 0.6 concatenate.3.ln_ref
  8.1 148.2 %first.1 = (bf16[512,768]{1,0:T(8,128)(2,1)}, f32[512,768]{1,0:T(8,128)}, bf16[4,512,768]{2,1,0:T(8,128)(2,1)}, f32[8,768]{1,0:T(8,128)}, f32[2,1152,768]{2,1,0:...) custom-call(s32[1,16]{1,0:T(1,128)} %lengths.1, ...), custom_call_target="tpu_custom_call" | custom-call | flops 10871635968 | bytes 15728640 | tf_op jit(solution)/shard_map/first/pallas_call | solution.py:594
  156.3 0.0 collective-permute-done.w_near_ref
  156.3 0.0 copy-start.2
  156.3 0.9 copy-done.2
  157.2 98.4 %back.1 = (bf16[512,768]{1,0:T(8,128)(2,1)}, bf16[2,384,768]{2,1,0:T(8,128)(2,1)}, bf16[2,1152,768]{2,1,0:T(8,128)(2,1)}, f32[8,768]{1,0:T(8,128)}) custom-call(bf16[4,192,512]{2,1,0:T(8,128)(2,1)} %get-tuple-element.32.att_ref, bf16[192,768]{1,0:T(8,128)(2,1)} %w_out_ref.1, f32[32,2048]{1,0:T(8,128)} %get-tuple-element.33.cos_ref, ...), custom_call_target="tpu_custom_call" | custom-call | flops 8053063680 | bytes 23592960 | tf_op jit(solution)/shard_map/back/pallas_call | solution.py:891
  255.7 0.0 copy-start
  255.7 0.0 copy-start.1
  255.7 8.3 %emit.1 = (f32[768,2,768]{2,1,0:T(2,128)}, f32[768,768]{1,0:T(8,128)}, f32[576,768]{1,0:T(8,128)}, f32[192,768]{1,0:T(8,128)}) custom-call(bf16[2,3,384,768]{3,2,1,0:T(8,128)(2,1)} %bitcast.13, bf16[2,384,768]{2,1,0:T(8,128)(2,1)} %get-tuple-element.46.small_ref), custom_call_target="tpu_custom_call" | custom-call | bytes 14155776 | tf_op jit(solution)/shard_map/emit/pallas_call | solution.py:962
  264.0 1.5 fusion
  265.5 0.0 copy-done
  265.5 0.9 copy.24
  266.4 0.0 copy-done.1
  266.4 0.9 copy.25
  (1 shorter events, 0.0 us)
Async XLA Ops:
  0.6 155.7 %collective-permute-start = (bf16[576,768]{1,0:T(8,128)(2,1)}, bf16[576,768]{1,0:T(8,128)(2,1)S(1)}, u32[]{:S(2)}, u32[]{:S(2)}) collective-permute-start(bf16[576,768]{1,0:T(8,128)(2,1)} %bitcast.21), channel_id=1, source_target_pairs={{0,1},{1,0},{2,3},{3,2},{4,5},{5,4},{6,7},{7,6},{8,9},{9,8},{10,11... | collective-permute-start | bytes 2654216 | tf_op jit(solution)/shard_map/ppermute | solution.py:996
  156.3 0.9 copy-start.2
  255.7 9.8 %copy-start = (bf16[512,768]{1,0:T(8,128)(2,1)S(1)}, bf16[512,768]{1,0:T(8,128)(2,1)}, u32[]{:S(2)}) copy-start(bf16[512,768]{1,0:T(8,128)(2,1)} %get-tuple-element.66) | copy-start | bytes 2359300
  255.7 10.7 %copy-start.1 = (bf16[512,768]{1,0:T(8,128)(2,1)S(1)}, bf16[512,768]{1,0:T(8,128)(2,1)}, u32[]{:S(2)}) copy-start(bf16[512,768]{1,0:T(8,128)(2,1)} %get-tuple-element.67) | copy-start | bytes 2359300

commit v2 on v1

--- a/solution.py
+++ b/solution.py
@@ -198,9 +198,9 @@
     ]
 
 
-X_FAR, X_NEAR, X_LAST, W_IN, W_DOWN, W_OUT, ATT = range(7)
-BRANCH, NORMED, OUT, DOUT, DNORMED, DH, DH_NEAR, DH_LAST, GRAD_NEAR = range(7, 16)
-KINDS = 16
+X_FAR, X_NEAR, X_LAST, W_IN, W_DOWN, W_OUT, ATT_NEAR, ATT_LAST = range(8)
+BRANCH, NORMED, OUT, DOUT, DNORMED, DH, DH_NEAR, DH_LAST, GRAD_NEAR = range(8, 17)
+KINDS = 17
 
 
 def first_kernel(
@@ -223,11 +223,18 @@
     ring_peers = Ring(size, me, give, None, None, None, None, None).peers
     greet([core, far] + [{"dp": peer} for peer in ring_peers])
 
+    def link(kind, c, source, target, partner):
+        return pltpu.make_async_remote_copy(
+            source, target, sems.at[0, kind, c], sems.at[1, kind, c], device_id=partner, device_id_type=MESH
+        )
+
     def post(kind, c, source, target, partner):
-        return send(source, target, sems.at[0, kind, c], sems.at[1, kind, c], partner)
-
-    far_copies = [post(X_FAR, c, tok_ref.at[where], x_ref.at[1, where], far) for c, where in enumerate(chunks)]
-    near_copy = post(X_NEAR, 0, tok_ref, x_ref.at[2], core)
+        copy = link(kind, c, source, target, partner)
+        copy.start()
+        return copy
+
+    far_copies = [post(X_FAR, c, tok_ref.at[where], x_ref.at[2, where], far) for c, where in enumerate(chunks)]
+    near_copy = post(X_NEAR, 0, tok_ref, x_ref.at[1], core)
     weight_copies = [
         post(W_OUT, 0, wo_ref, wo_near_ref, core),
         post(W_IN, 0, win_hbm, win.at[1], core),
@@ -241,15 +248,34 @@
     sums[...] = jnp.zeros_like(sums)
     scale_one, shift_one, scale_two, shift_two = (ln_ref[i : i + 1, :] for i in range(4))
 
-    def exchange(kind, value_of):
-        copies = []
-        for c, where in enumerate(chunks):
-            outbox[where, :] = value_of(where).astype(BF16)
-            copies.append(post(kind, c, outbox.at[where], inbox.at[where], far))
-        return copies
-
-    def branch(index, where):
-        return mm(att[index, :, where], wo_ref[...], TN) + mm(near[index, :, where], wo_near_ref[...], TN)
+    def branch(slot, other, where):
+        return mm(att[slot, :, where], wo_ref[...], TN) + mm(near[other, :, where], wo_near_ref[...], TN)
+
+    def by_parts(c, part):
+        step = 64
+
+        def run(i, carry):
+            part(pl.ds(pl.multiple_of(c * chunk + i * step, step), step))
+            return carry
+
+        lax.fori_loop(0, chunk // step, run, 0)
+
+    def mean(values):
+        return jnp.sum(values, axis=-1, keepdims=True) * (1.0 / width)
+
+    def add_up(index, values):
+        sums[index] += jnp.sum(values.reshape(values.shape[0] // 8, 8, width), axis=0)
+
+    def norm_one(where):
+        h = hat[where, :] + inbox[where, :].astype(F32)
+        h = h - mean(h)
+        r = lax.rsqrt(mean(h * h) + EPSILON)
+        h = h * r
+        hat[where, :] = h
+        r1[where, :] = jnp.broadcast_to(r, (r.shape[0], LANES))
+        h = h * scale_one + shift_one
+        res[where, :] = h
+        low[0, where, :] = h.astype(BF16)
 
     def attention(q_ref, k_ref, v_ref, k_rows_ref, q_rows_ref, cos_ref, sin_ref, top_ref, acc_ref):
         half_head = HEAD_DIM // 2
@@ -272,7 +298,7 @@
 
         def tables(slot):
             where = slice(slot * rows, (slot + 1) * rows)
-            shard = 2 * ((slot % 2 + m // 2) % 2) + (slot // 2 + m) % 2
+            shard = 2 * ((slot // 2 + m // 2) % 2) + (slot + m) % 2
             token = lax.broadcasted_iota(jnp.int32, (16, rows), 1) + shard * rows
             inside = (token >= first) & (token < last)
             begin = jnp.max(jnp.where(inside, first, 0), axis=0, keepdims=True)
@@ -285,9 +311,9 @@
                 k_ref[h, HEAD_DIM:, where] = jnp.concatenate([jnp.where(inside, 1.0, 0.0), ones], axis=0).astype(BF16)
                 v_ref[h, HEAD_DIM:, where] = v_tail.astype(BF16)
 
-        def project(slot):
-            where = slice(slot * rows, (slot + 1) * rows)
-            projected = mm(w_ref[...], x_ref[slot], NT)
+        def project(slot, c):
+            where = slice(slot * rows + c * chunk, slot * rows + (c + 1) * chunk)
+            projected = mm(w_ref[...], x_ref[slot, chunks[c], :], NT)
             cosine, sine = cos_ref[:, where], sin_ref[:, where]
 
             def rotated(start, scale):
@@ -306,15 +332,18 @@
 
         def pairs(count, pair):
             def run(n, carry):
-                qs, ks = pair(n)
-                queries, keys = span(qs, rows), span(ks, rows)
+                qs, group = pair(n)
+                queries, keys = span(qs, chunk), span(group, 2 * rows)
+                scores, olds, tops = [], [], []
                 for h in range(heads):
                     s = mm(k_rows_ref[h, keys, :], q_ref[h, :, queries])
-                    old = top_ref[qs, h, 0:1, :]
-                    top = jnp.maximum(old, jnp.max(s, axis=0, keepdims=True))
-                    probs = jnp.exp2(s - top).astype(BF16)
-                    top_ref[qs, h, 0:1, :] = top
-                    acc_ref[qs, h] = acc_ref[qs, h] * jnp.exp2(old - top) + mm(v_ref[h, :80, keys], probs)
+                    olds.append(top_ref[qs, h, 0:1, :])
+                    tops.append(jnp.maximum(olds[h], jnp.max(s, axis=0, keepdims=True)))
+                    scores.append(s)
+                for h in range(heads):
+                    probs = jnp.exp2(scores[h] - tops[h]).astype(BF16)
+                    top_ref[qs, h, 0:1, :] = tops[h]
+                    acc_ref[qs, h] = acc_ref[qs, h] * jnp.exp2(olds[h] - tops[h]) + mm(v_ref[h, :80, keys], probs)
                 return carry
 
             lax.fori_loop(0, count, run, 0)
@@ -325,52 +354,75 @@
             writes.append(pltpu.make_async_copy(source, target, stores.at[len(writes)]))
             writes[-1].start()
 
-        def settle(slot):
-            where = slice(slot * rows, (slot + 1) * rows)
+        def settle(slot, c):
+            part = 2 * slot + c
             for h in range(heads):
-                total = acc_ref[slot, h, HEAD_DIM : HEAD_DIM + 1, :]
-                out = acc_ref[slot, h, :HEAD_DIM, :] / total
-                att[slot, h * HEAD_DIM : (h + 1) * HEAD_DIM, :] = out.astype(BF16)
-                level = top_ref[slot, h, 0:1, :] + jnp.log2(total)
+                total = acc_ref[part, h, HEAD_DIM : HEAD_DIM + 1, :]
+                out = acc_ref[part, h, :HEAD_DIM, :] / total
+                att[slot, h * HEAD_DIM : (h + 1) * HEAD_DIM, chunks[c]] = out.astype(BF16)
+                top_ref[part, h, 1:2, :] = top_ref[part, h, 0:1, :] + jnp.log2(total)
+
+        def turn(part, carry):
+            where = span(part, chunk)
+            for h in range(heads):
                 query = q_ref[h, :, where].astype(F32)
-                wide = jnp.concatenate([query[:80], thirds(-level), query[96:]], axis=0)
+                wide = jnp.concatenate([query[:80], thirds(-top_ref[part, h, 1:2, :]), query[96:]], axis=0)
                 q_rows_ref[h, where, :] = wide.T.astype(BF16)
+            return carry
 
         for slot in range(4):
             tables(slot)
-        project(0)
+        last_copies = []
+
+        def hand_on(c):
+            far_copies[c].wait()
+            last_copies.append(post(X_LAST, c, x_ref.at[2, chunks[c]], x_ref.at[3, chunks[c]], core))
+
+        for c in range(2):
+            project(0, c)
         near_copy.wait()
-        project(2)
-        pairs(4, lambda n: (2 * (n // 2), 2 * (n % 2)))
-        last_copies = []
-        for c, where in enumerate(chunks):
-            far_copies[c].wait()
-            last_copies.append(post(X_LAST, c, x_ref.at[1, where], x_ref.at[3, where], core))
-        project(1)
-        for copy in last_copies:
-            copy.wait()
-        project(3)
+        for c in range(2):
+            project(1, c)
+        hand_on(0)
+        pairs(4, lambda n: (n, 0))
+        project(2, 0)
+        last_copies[0].wait()
+        project(3, 0)
+        hand_on(1)
+        project(2, 1)
+        last_copies[1].wait()
+        project(3, 1)
         for source, target in [
             (x_ref, x_hbm), (q_ref, q_hbm), (k_ref, k_hbm), (v_ref, v_hbm), (cos_ref, cos_hbm), (sin_ref, sin_hbm)
         ]:
             write(source, target)
-        pairs(4, lambda n: (3, n))
-        settle(3)
-        copies = [post(ATT, 1, att.at[3], near.at[1], core)]
-        pairs(4, lambda n: (1, n))
-        settle(1)
         weight_copies[0].wait()
-        copies[0].wait()
-        exchange(BRANCH, lambda where: branch(1, where))
-        pairs(4, lambda n: (2 * (1 - n // 2), 2 * (n % 2) + 1))
-        settle(2)
-        copies.append(post(ATT, 0, att.at[2], near.at[0], core))
-        settle(0)
+        branch_copies = []
+        for c, where in enumerate(chunks):
+            pairs(2, lambda n: (6 + c, n))
+            settle(3, c)
+            last_att = post(ATT_LAST, c, att.at[3, :, where], near.at[1, :, where], core)
+            pairs(2, lambda n: (4 + c, n))
+            settle(2, c)
+            last_att.wait()
+            outbox[where, :] = branch(2, 1, where).astype(BF16)
+            branch_copies.append(post(BRANCH, c, outbox.at[where], inbox.at[where], far))
+        pairs(4, lambda n: (3 - n, 1))
+        for c in range(2):
+            settle(1, c)
+        near_att = post(ATT_NEAR, 0, att.at[1], near.at[0], core)
+        for c in range(2):
+            settle(0, c)
+        write(att, att_hbm)
+        near_att.wait()
+        for where in chunks:
+            hat[where, :] = tok_ref[where, :].astype(F32) + branch(0, 0, where)
+        for c, where in enumerate(chunks):
+            branch_copies[c].wait()
+            by_parts(c, norm_one)
+            post(NORMED, c, low.at[0, where], low.at[1, where], far)
+        lax.fori_loop(0, 2 * shards, turn, 0)
         write(q_rows_ref, q_rows_hbm)
-        write(att, att_hbm)
-        copies[1].wait()
-        for where in chunks:
-            hat[where, :] = tok_ref[where, :].astype(F32) + branch(0, where)
         for copy in writes:
             copy.wait()
 
@@ -379,51 +431,9 @@
     table = pltpu.VMEM((HEAD_DIM // 2, tokens), F32)
     pl.run_scoped(
         attention, along, along, along, down, down, table, table,
-        pltpu.VMEM((shards, heads, 8, rows), F32), pltpu.VMEM((shards, heads, 80, rows), F32),
+        pltpu.VMEM((2 * shards, heads, 8, chunk), F32), pltpu.VMEM((2 * shards, heads, 80, chunk), F32),
     )
-    branch_copies = [
-        pltpu.make_async_remote_copy(
-            outbox.at[where],
-            inbox.at[where],
-            sems.at[0, BRANCH, c],
-            sems.at[1, BRANCH, c],
-            device_id=far,
-            device_id_type=MESH,
-        )
-        for c, where in enumerate(chunks)
-    ]
-
-    def by_parts(c, part):
-        step = 64
-
-        def run(i, carry):
-            part(pl.ds(pl.multiple_of(c * chunk + i * step, step), step))
-            return carry
-
-        lax.fori_loop(0, chunk // step, run, 0)
-
-    def mean(values):
-        return jnp.sum(values, axis=-1, keepdims=True) * (1.0 / width)
-
-    def add_up(index, values):
-        sums[index] += jnp.sum(values.reshape(values.shape[0] // 8, 8, width), axis=0)
-
-    def norm_one(where):
-        h = hat[where, :] + inbox[where, :].astype(F32)
-        h = h - mean(h)
-        r = lax.rsqrt(mean(h * h) + EPSILON)
-        h = h * r
-        hat[where, :] = h
-        r1[where, :] = jnp.broadcast_to(r, (r.shape[0], LANES))
-        h = h * scale_one + shift_one
-        res[where, :] = h
-        low[0, where, :] = h.astype(BF16)
-
-    normed_copies = []
-    for c, where in enumerate(chunks):
-        branch_copies[c].wait()
-        by_parts(c, norm_one)
-        normed_copies.append(post(NORMED, c, low.at[0, where], low.at[1, where], far))
+    normed_copies = [link(NORMED, c, low.at[0, where], low.at[1, where], far) for c, where in enumerate(chunks)]
     for copy in fetches + weight_copies[1:]:
         copy.wait()
 
@@ -512,14 +522,7 @@
             lax.fori_loop(0, 2, chain, 0)
 
         def grad_copy(r):
-            return pltpu.make_async_remote_copy(
-                give.at[r],
-                take.at[r],
-                sems.at[0, GRAD_NEAR, r],
-                sems.at[1, GRAD_NEAR, r],
-                device_id=core,
-                device_id_type=MESH,
-            )
+            return link(GRAD_NEAR, r, give.at[r], take.at[r], core)
 
         weight_grads(1, give, lambda r: grad_copy(r).start())
 
@@ -540,8 +543,8 @@
             dnormed_copies[c].wait()
             by_parts(c, norm_one_back)
             mine = slots_ref.at[0, where]
-            dh_copies.append(post(DH, c, mine, slots_ref.at[1, where], far))
-            last_copies.append(post(DH_NEAR, c, mine, slots_ref.at[2, where], core))
+            dh_copies.append(post(DH, c, mine, slots_ref.at[2, where], far))
+            last_copies.append(post(DH_NEAR, c, mine, slots_ref.at[1, where], core))
 
         dh_chunk(0)
         weight_grads(0, total)
@@ -554,16 +557,18 @@
         def hand_on(c):
             dh_copies[c].wait()
             where = chunks[c]
-            last_copies.append(post(DH_LAST, c, slots_ref.at[1, where], slots_ref.at[3, where], core))
+            last_copies.append(post(DH_LAST, c, slots_ref.at[2, where], slots_ref.at[3, where], core))
 
         for i in range(4):
             norms_ref[i : i + 1, :] = jnp.sum(sums[i], axis=0, keepdims=True)
         norms_ref[4:8, :] = jnp.zeros((4, width), F32)
-        hand_on(0)
         for step in range(RING_EARLY - 1):
             for sub in range(2):
                 ring.pass_on(step, sub)
-        hand_on(1)
+            if step < 2:
+                hand_on(step)
+        for step in range(RING_EARLY - 1, 2):
+            hand_on(step)
         ring.keep(RING_EARLY - 1)
         write = pltpu.make_async_copy(total, total_hbm, loads.at[0])
         write.start()
@@ -824,7 +829,7 @@
         for h in range(heads):
             pieces += rotated_back(dq_ref[h, :, span(i, rows)], cosine, sine)
         d_qkv[i, :cols, :] = jnp.concatenate(pieces, axis=0).astype(BF16)
-    near_copy = send(d_qkv.at[pl.ds(2, 2)], near, near_sem.at[0], near_sem.at[1], core)
+    near_copies = [send(d_qkv.at[2 * i + 1], near.at[i], near_sem.at[0, i], near_sem.at[1, i], core) for i in range(2)]
 
     def product(first, count):
         piece = mm(d_qkv[0, first : first + count, :], x_ref[0])
@@ -845,10 +850,11 @@
         return send(sums_ref, norm_in.at[stage], norm_sem.at[0, stage], norm_sem.at[1, stage], partners[stage])
 
     norm_copy, norm_done = norm_exchange(0), 0
-    near_copy.wait()
+    for copy in near_copies:
+        copy.wait()
 
     def d_tokens(index):
-        return mm(d_qkv[index], w_ref[...], TN) + mm(near[index], w_near_ref[...], TN)
+        return mm(d_qkv[2 * index], w_ref[...], TN) + mm(near[index], w_near_ref[...], TN)
 
     far_out[...] = d_tokens(1).astype(BF16)
     far_copy = send(far_out, far_in, far_sem.at[0], far_sem.at[1], far)
@@ -923,7 +929,7 @@
             *ring_scratch(size, big_chain, width, ring_steps),
             dma((2, 2, 2, spots - 1)),
             dma((7,)),
-            dma((2,)),
+            dma((2, 2)),
             dma((2,)),
             dma((2, 2, steps)),
             dma((2, 2 + stages)),
@@ -938,27 +944,56 @@
     )(att, w_out, cosine, sine, norms, w_turned, w_near, dh, totals, dh_slots, q_rows, q, k, v, x_slots)
 
 
-def emit_kernel(big_ref, small_ref, gate_up_ref, down_ref, qkv_ref, out_ref):
+def emit_kernel(big_ref, small_ref, out_ref, dx_ref, gate_up_hbm, down_ref, qkv_ref, w_out_ref, out_copy_ref, dx_copy_ref, wide, sems):
+    step, steps = pl.program_id(0), pl.num_programs(0)
+    rows = down_ref.shape[0]
+
+    def copies(which):
+        return [
+            pltpu.make_async_copy(
+                wide.at[which % 2, n], gate_up_hbm.at[span(which, rows), n, :], sems.at[which % 2, n]
+            )
+            for n in range(2)
+        ]
+
+    @pl.when(step >= 2)
+    def _():
+        for copy in copies(step - 2):
+            copy.wait()
+
     for n in range(2):
-        gate_up_ref[:, n, :] = big_ref[0, n].astype(F32)
+        wide[step % 2, n] = big_ref[0, n].astype(F32)
+    for copy in copies(step):
+        copy.start()
     down_ref[...] = big_ref[0, 2].astype(F32)
-    qkv_steps = pl.num_programs(0) * 3 // 4
-
-    @pl.when(pl.program_id(0) < qkv_steps)
+    out_copy_ref[...] = out_ref[...]
+    dx_copy_ref[...] = dx_ref[...]
+    qkv_steps = steps * 3 // 4
+
+    @pl.when(step < qkv_steps)
     def _():
         qkv_ref[...] = small_ref[0].astype(F32)
 
-    @pl.when(pl.program_id(0) >= qkv_steps)
+    @pl.when(step >= qkv_steps)
     def _():
-        out_ref[...] = small_ref[0].astype(F32)
-
-
-def emit(big, small):
+        w_out_ref[...] = small_ref[0].astype(F32)
+
+    @pl.when(step == steps - 1)
+    def _():
+        for which in (steps - 2, steps - 1):
+            for copy in copies(which):
+                copy.wait()
+
+
+def emit(big, small, output, d_tokens):
     _, chain, width = small.shape
     steps = 8
     per, rows = steps // 2, width // steps
     qkv_steps = steps * 3 // 4
+    tokens = output.shape[0] // steps
     shape = lambda *dims: jax.ShapeDtypeStruct(dims, F32)
+    low = jax.ShapeDtypeStruct(output.shape, BF16)
+    few = pl.BlockSpec((tokens, width), lambda i: (i, 0))
     return pl.pallas_call(
         emit_kernel,
         out_shape=(
@@ -966,22 +1001,29 @@
             shape(width, width),
             shape(qkv_steps * rows, width),
             shape((steps - qkv_steps) * rows, width),
+            low,
+            low,
         ),
         grid=(steps,),
         in_specs=[
             pl.BlockSpec((1, 3, rows, width), lambda i: (i // per, 0, i % per, 0)),
             pl.BlockSpec((1, rows, width), lambda i: (i // per, i % per, 0)),
+            few,
+            few,
         ],
         out_specs=[
-            pl.BlockSpec((rows, 2, width), lambda i: (i, 0, 0)),
+            pl.BlockSpec(memory_space=pl.ANY),
             pl.BlockSpec((rows, width), lambda i: (i, 0)),
             pl.BlockSpec((rows, width), lambda i: (jnp.minimum(i, qkv_steps - 1), 0)),
             pl.BlockSpec((rows, width), lambda i: (jnp.maximum(i - qkv_steps, 0), 0)),
+            few,
+            few,
         ],
+        scratch_shapes=[pltpu.VMEM((2, 2, rows, width), F32), pltpu.SemaphoreType.DMA((2, 2))],
         compiler_params=pltpu.CompilerParams(vmem_limit_bytes=VMEM_LIMIT),
         cost_estimate=pl.CostEstimate(flops=0, bytes_accessed=24 * width * width, transcendentals=0),
         name="emit",
-    )(big.reshape(2, 3, chain, width), small)
+    )(big.reshape(2, 3, chain, width), small, output, d_tokens)
 
 
 def body(
@@ -1001,7 +1043,7 @@
     d_tokens, small, big, norms = back(
         att, w_out, cosine, sine, norms, qkv_turned, qkv_near, dh, totals, dh_slots, q_rows, q, k, v, x_slots
     )
-    grad_gate_up, grad_down, grad_qkv, grad_out = emit(big, small)
+    grad_gate_up, grad_down, grad_qkv, grad_out, output, d_tokens = emit(big, small, output, d_tokens)
     grad_qkv = grad_qkv.reshape(3, local_cols, width).transpose(2, 0, 1)
     norms = lax.dynamic_slice_in_dim(norms, m * local_cols, local_cols, 1)
     return (

time: 268 us -> 260 us (0.970); the launches traced: 267 us -> 257 us
  Pallas kernels: 255 us -> 248 us
  local copies, waits for them, and re-layouts: 11.1 us -> 6.65 us
    pallas_call x1, Pallas kernels: 148 us -> 141 us  [first(): pl.pallas_call(functools.partial(first_kernel, size), out_shape=(shape((r...]
    another operation x4, local copies, waits for them, and re-layouts: 2.76 us -> 0.02 us  [body(): jnp.stack([ln1_scale, ln1_shift, ln2_scale, ln2_shift])]
    unnamed x9 -> x11, local copies, waits for them, and re-layouts: 6.17 us -> 4.47 us
  transfers between devices with their start and end apart: 1 -> 1, of which waited for: 0 -> 0; matrix products, arithmetic and copies ran while one was open for 3% -> 2% of each run, Pallas kernels for 55% -> 55%
where the time goes in v2:
time: 260 us; the launch traced here: 257 us
  Pallas kernels  248 us (95%)
  local copies, waits for them, and re-layouts  6.65 us (3%)
    pallas_call x1, Pallas kernels, first(): pl.pallas_call(functools.partial(first_kernel, size), out_shape=(shape((r...  141 us
    pallas_call x1, Pallas kernels, back(): pl.pallas_call(functools.partial(back_kernel, size), out_shape=(jax.Shape...  98.2 us
    pallas_call x1, Pallas kernels, emit(): pl.pallas_call(emit_kernel, out_shape=(shape(width, 2, width), shape(widt...  9.23 us
  transfers between devices with their start and end apart: 1, of which 0 were waited for; matrix products, arithmetic and copies ran while one was open for 2% of the time, Pallas kernels for 55%

profile of v2, /device:TPU:0, one launch (start us, length us, event | category | flops | bytes accessed | tf_op | source)
XLA Modules:
  0.0 256.6 jit_solution(14329975044518077138)
XLA Ops:
  0.6 0.5 collective-permute-start
  1.2 0.0 copy-start
  1.2 0.0 copy-start.1
  1.2 0.0 copy-start.2
  1.2 0.0 copy-start.3
  1.2 3.6 %copy.21 = bf16[96,8,2,768]{3,1,2,0:T(8,128)(2,1)} copy(bf16[96,8,2,768]{3,2,1,0:T(2,128)(2,1)} %bitcast.14) | data formatting | bytes 4718592
  4.7 0.0 copy-done
  4.7 0.0 copy-done.1
  4.7 0.0 copy-done.2
  4.8 0.0 copy-done.3
  4.8 0.6 concatenate.3.ln_ref
  5.4 140.8 %first.1 = (bf16[512,768]{1,0:T(8,128)(2,1)}, f32[512,768]{1,0:T(8,128)}, bf16[4,512,768]{2,1,0:T(8,128)(2,1)}, f32[8,768]{1,0:T(8,128)}, f32[2,1152,768]{2,1,0:...) custom-call(s32[1,16]{1,0:T(1,128)} %lengths.1, ...), custom_call_target="tpu_custom_call" | custom-call | flops 10871635968 | bytes 15728640 | tf_op jit(solution)/shard_map/first/pallas_call | solution.py:599
  146.2 0.0 collective-permute-done.w_near_ref
  146.2 0.0 copy-start.4
  146.2 0.9 copy-done.4
  147.1 98.2 %back.1 = (bf16[512,768]{1,0:T(8,128)(2,1)}, bf16[2,384,768]{2,1,0:T(8,128)(2,1)}, bf16[2,1152,768]{2,1,0:T(8,128)(2,1)}, f32[8,768]{1,0:T(8,128)}) custom-call(bf16[4,192,512]{2,1,0:T(8,128)(2,1)} %get-tuple-element.33.att_ref, bf16[192,768]{1,0:T(8,128)(2,1)} %w_out_ref.1, f32[32,2048]{1,0:T(8,128)} %get-tuple-element.34.cos_ref, ...), custom_call_target="tpu_custom_call" | custom-call | flops 8053063680 | bytes 23592960 | tf_op jit(solution)/shard_map/back/pallas_call | solution.py:897
  245.4 9.2 %emit.1 = (f32[768,2,768]{2,1,0:T(2,128)}, f32[768,768]{1,0:T(8,128)}, f32[576,768]{1,0:T(8,128)}, f32[192,768]{1,0:T(8,128)}, bf16[512,768]{1,0:T(8,128)(2,1)}, /*index=5*/bf16[512,768]{1,0:T(8,128)(2,1)}) custom-call(bf16[2,3,384,768]{3,2,1,0:T(8,128)(2,1)} %bitcast.13, bf16[2,384,768]{2,1,0:T(8,128)(2,1)} %get-tuple-element.46.small_ref, ...), custom_call_target="tpu_custom_call" | custom-call | bytes 14155776 | tf_op jit(solution)/shard_map/emit/pallas_call | solution.py:997
  254.6 1.5 fusion
  (5 shorter events, 0.0 us)
Async XLA Ops:
  0.6 145.6 %collective-permute-start = (bf16[576,768]{1,0:T(8,128)(2,1)}, bf16[576,768]{1,0:T(8,128)(2,1)S(1)}, u32[]{:S(2)}, u32[]{:S(2)}) collective-permute-start(bf16[576,768]{1,0:T(8,128)(2,1)} %bitcast.21), channel_id=1, source_target_pairs={{0,1},{1,0},{2,3},{3,2},{4,5},{5,4},{6,7},{7,6},{8,9},{9,8},{10,11... | collective-permute-start | bytes 2654216 | tf_op jit(solution)/shard_map/ppermute | solution.py:1038
  1.2 3.6 %copy-start = (f32[768]{0:T(1024)S(1)}, f32[768]{0:T(1024)}, u32[]{:S(2)}) copy-start(f32[768]{0:T(1024)} %param.17) | copy-start | bytes 9220
  1.2 3.6 %copy-start.1 = (f32[768]{0:T(1024)S(1)}, f32[768]{0:T(1024)}, u32[]{:S(2)}) copy-start(f32[768]{0:T(1024)} %param.18) | copy-start | bytes 9220
  1.2 3.6 %copy-start.2 = (f32[768]{0:T(1024)S(1)}, f32[768]{0:T(1024)}, u32[]{:S(2)}) copy-start(f32[768]{0:T(1024)} %param.19) | copy-start | bytes 9220
  1.2 3.6 %copy-start.3 = (f32[768]{0:T(1024)S(1)}, f32[768]{0:T(1024)}, u32[]{:S(2)}) copy-start(f32[768]{0:T(1024)} %param.20) | copy-start | bytes 9220
  146.2 0.9 copy-start.4

commit v3 on v2

--- a/solution.py
+++ b/solution.py
@@ -237,11 +237,10 @@
     near_copy = post(X_NEAR, 0, tok_ref, x_ref.at[1], core)
     weight_copies = [
         post(W_OUT, 0, wo_ref, wo_near_ref, core),
-        post(W_IN, 0, win_hbm, win.at[1], core),
         post(W_DOWN, 0, wdn_hbm, wdn.at[pl.ds(hidden, hidden)], core),
     ]
     fetches = []
-    for n, (source, target) in enumerate([(win_hbm, win.at[0]), (wdn_hbm, wdn.at[pl.ds(0, hidden)])]):
+    for n, (source, target) in enumerate([(wdn_hbm, wdn.at[pl.ds(0, hidden)])]):
         fetches.append(pltpu.make_async_copy(source, target, loads.at[n]))
         fetches[-1].start()
     x_ref[0] = tok_ref[...]
@@ -277,7 +276,9 @@
         res[where, :] = h
         low[0, where, :] = h.astype(BF16)
 
-    def attention(q_ref, k_ref, v_ref, k_rows_ref, q_rows_ref, cos_ref, sin_ref, top_ref, acc_ref):
+    def attention(raw, q_ref, k_ref, v_ref, k_rows_ref, q_rows_ref, cos_ref, sin_ref, top_ref, acc_ref):
+        fetch = pltpu.make_async_copy(win_hbm, raw, loads.at[1])
+        fetch.start()
         half_head = HEAD_DIM // 2
         starts, ends, end = [], [], 0
         for d in range(lengths.shape[1]):
@@ -296,8 +297,8 @@
         top_ref[...] = jnp.full_like(top_ref, FAR)
         acc_ref[...] = jnp.zeros_like(acc_ref)
 
-        def tables(slot):
-            where = slice(slot * rows, (slot + 1) * rows)
+        def tables(slot, carry):
+            where = span(slot, rows)
             shard = 2 * ((slot // 2 + m // 2) % 2) + (slot + m) % 2
             token = lax.broadcasted_iota(jnp.int32, (16, rows), 1) + shard * rows
             inside = (token >= first) & (token < last)
@@ -310,10 +311,11 @@
                 ).astype(BF16)
                 k_ref[h, HEAD_DIM:, where] = jnp.concatenate([jnp.where(inside, 1.0, 0.0), ones], axis=0).astype(BF16)
                 v_ref[h, HEAD_DIM:, where] = v_tail.astype(BF16)
-
-        def project(slot, c):
-            where = slice(slot * rows + c * chunk, slot * rows + (c + 1) * chunk)
-            projected = mm(w_ref[...], x_ref[slot, chunks[c], :], NT)
+            return carry
+
+        def project(part, carry):
+            where = span(part, chunk)
+            projected = mm(w_ref[...], x_ref[part // 2, span(part % 2, chunk), :], NT)
             cosine, sine = cos_ref[:, where], sin_ref[:, where]
 
             def rotated(start, scale):
@@ -329,6 +331,7 @@
                 k_rows_ref[h, where, :] = jnp.concatenate([k, tail], axis=0).T.astype(BF16)
                 start = 2 * cols + h * HEAD_DIM
                 v_ref[h, :HEAD_DIM, where] = projected[start : start + HEAD_DIM].astype(BF16)
+            return carry
 
         def pairs(count, pair):
             def run(n, carry):
@@ -370,28 +373,33 @@
                 q_rows_ref[h, where, :] = wide.T.astype(BF16)
             return carry
 
-        for slot in range(4):
-            tables(slot)
+        lax.fori_loop(0, shards, tables, 0)
+        fetch.wait()
+
+        def untangle(i, carry):
+            where = span(i, 32)
+            for n in range(2):
+                win[0, where, n * hidden : (n + 1) * hidden] = raw[where, n, :]
+            return carry
+
+        lax.fori_loop(0, width // 32, untangle, 0)
+        post(W_IN, 0, win.at[0], win.at[1], core)
         last_copies = []
 
         def hand_on(c):
             far_copies[c].wait()
             last_copies.append(post(X_LAST, c, x_ref.at[2, chunks[c]], x_ref.at[3, chunks[c]], core))
 
-        for c in range(2):
-            project(0, c)
         near_copy.wait()
-        for c in range(2):
-            project(1, c)
+        lax.fori_loop(0, 4, project, 0)
         hand_on(0)
         pairs(4, lambda n: (n, 0))
-        project(2, 0)
         last_copies[0].wait()
-        project(3, 0)
+        lax.fori_loop(0, 2, lambda n, carry: project(4 + 2 * n, carry), 0)
         hand_on(1)
-        project(2, 1)
+        project(5, 0)
         last_copies[1].wait()
-        project(3, 1)
+        project(7, 0)
         for source, target in [
             (x_ref, x_hbm), (q_ref, q_hbm), (k_ref, k_hbm), (v_ref, v_hbm), (cos_ref, cos_hbm), (sin_ref, sin_hbm)
         ]:
@@ -430,11 +438,11 @@
     down = pltpu.VMEM((heads, tokens, LANES), BF16)
     table = pltpu.VMEM((HEAD_DIM // 2, tokens), F32)
     pl.run_scoped(
-        attention, along, along, along, down, down, table, table,
+        attention, pltpu.VMEM((width, 2, hidden), BF16), along, along, along, down, down, table, table,
         pltpu.VMEM((2 * shards, heads, 8, chunk), F32), pltpu.VMEM((2 * shards, heads, 80, chunk), F32),
     )
     normed_copies = [link(NORMED, c, low.at[0, where], low.at[1, where], far) for c, where in enumerate(chunks)]
-    for copy in fetches + weight_copies[1:]:
+    for copy in fetches + weight_copies[1:] + [link(W_IN, 0, win.at[0], win.at[1], core)]:
         copy.wait()
 
     def feed_forward(gu, hid, total):
@@ -701,9 +709,9 @@
             device_id_type=MESH,
         )
 
-    def start(self, index):
+    def start(self, index, chains=(0, 1)):
         step = self.steps[index]
-        for chain in range(2):
+        for chain in chains:
             if step["kind"] != "gather":
                 spot = pl.ds(step["spot"] * self.rows, step["part"] * self.rows)
                 away = self.block(step["chains"][chain]["away"], step["part"])
@@ -950,19 +958,12 @@
 
     def copies(which):
         return [
-            pltpu.make_async_copy(
-                wide.at[which % 2, n], gate_up_hbm.at[span(which, rows), n, :], sems.at[which % 2, n]
-            )
+            pltpu.make_async_copy(wide.at[which, n], gate_up_hbm.at[span(which, rows), n, :], sems.at[which, n])
             for n in range(2)
         ]
 
-    @pl.when(step >= 2)
-    def _():
-        for copy in copies(step - 2):
-            copy.wait()
-
     for n in range(2):
-        wide[step % 2, n] = big_ref[0, n].astype(F32)
+        wide[step, n] = big_ref[0, n].astype(F32)
     for copy in copies(step):
         copy.start()
     down_ref[...] = big_ref[0, 2].astype(F32)
@@ -980,7 +981,7 @@
 
     @pl.when(step == steps - 1)
     def _():
-        for which in (steps - 2, steps - 1):
+        for which in range(steps):
             for copy in copies(which):
                 copy.wait()
 
@@ -1019,7 +1020,7 @@
             few,
             few,
         ],
-        scratch_shapes=[pltpu.VMEM((2, 2, rows, width), F32), pltpu.SemaphoreType.DMA((2, 2))],
+        scratch_shapes=[pltpu.VMEM((steps, 2, rows, width), F32), pltpu.SemaphoreType.DMA((steps, 2))],
         compiler_params=pltpu.CompilerParams(vmem_limit_bytes=VMEM_LIMIT),
         cost_estimate=pl.CostEstimate(flops=0, bytes_accessed=24 * width * width, transcendentals=0),
         name="emit",
@@ -1038,7 +1039,7 @@
     qkv_near = lax.ppermute(qkv_turned, "mp", [(i, i ^ 1) for i in range(shards)])
     norms = jnp.concatenate([jnp.stack([ln1_scale, ln1_shift, ln2_scale, ln2_shift]), jnp.zeros((4, width), F32)])
     output, dh, dh_slots, norms, totals, x_slots, q, k, v, q_rows, att, cosine, sine = first(
-        lengths, tokens, cotangent, norms, qkv_turned, w_out, w_gate_up.reshape(width, 2 * hidden_cols), w_down
+        lengths, tokens, cotangent, norms, qkv_turned, w_out, w_gate_up, w_down
     )
     d_tokens, small, big, norms = back(
         att, w_out, cosine, sine, norms, qkv_turned, qkv_near, dh, totals, dh_slots, q_rows, q, k, v, x_slots

time: 260 us -> 256 us (0.985); the launches traced: 257 us -> 255 us
    unnamed x11 -> x2, local copies, waits for them, and re-layouts: 4.47 us -> 0.91 us
    another operation x4, local copies, waits for them, and re-layouts: 0.02 us -> 2.76 us  [body(): jnp.stack([ln1_scale, ln1_shift, ln2_scale, ln2_shift])]
  transfers between devices with their start and end apart: 1 -> 1, of which waited for: 0 -> 0; matrix products, arithmetic and copies ran while one was open for 2% -> 1% of each run, Pallas kernels for 55% -> 55%
where the time goes in v3:
time: 256 us; the launch traced here: 255 us
  Pallas kernels  248 us (97%)
  local copies, waits for them, and re-layouts  5.82 us (2%)
    pallas_call x1, Pallas kernels, first(): pl.pallas_call(functools.partial(first_kernel, size), out_shape=(shape((r...  141 us
    pallas_call x1, Pallas kernels, back(): pl.pallas_call(functools.partial(back_kernel, size), out_shape=(jax.Shape...  98.2 us
    pallas_call x1, Pallas kernels, emit(): pl.pallas_call(emit_kernel, out_shape=(shape(width, 2, width), shape(widt...  9.38 us
  transfers between devices with their start and end apart: 1, of which 0 were waited for; matrix products, arithmetic and copies ran while one was open for 1% of the time, Pallas kernels for 55%

profile of v3, /device:TPU:0, one launch (start us, length us, event | category | flops | bytes accessed | tf_op | source)
XLA Modules:
  0.0 255.4 jit_solution(16308010828236047417)
XLA Ops:
  0.6 0.5 collective-permute-start
  1.2 0.7 stack.12
  1.8 0.7 stack.13
  2.5 0.7 stack.14
  3.2 0.7 stack.15
  3.9 0.6 concatenate.3.ln_ref
  4.6 140.7 %first.1 = (bf16[512,768]{1,0:T(8,128)(2,1)}, f32[512,768]{1,0:T(8,128)}, bf16[4,512,768]{2,1,0:T(8,128)(2,1)}, f32[8,768]{1,0:T(8,128)}, f32[2,1152,768]{2,1,0:...) custom-call(s32[1,16]{1,0:T(1,128)} %lengths.1, ...), custom_call_target="tpu_custom_call" | custom-call | flops 10871635968 | bytes 15728640 | tf_op jit(solution)/shard_map/first/pallas_call | solution.py:607
  145.3 0.0 collective-permute-done.w_near_ref
  145.3 0.0 copy-start
  145.3 0.9 copy-done
  146.2 98.2 %back.1 = (bf16[512,768]{1,0:T(8,128)(2,1)}, bf16[2,384,768]{2,1,0:T(8,128)(2,1)}, bf16[2,1152,768]{2,1,0:T(8,128)(2,1)}, f32[8,768]{1,0:T(8,128)}) custom-call(bf16[4,192,512]{2,1,0:T(8,128)(2,1)} %get-tuple-element.33.att_ref, bf16[192,768]{1,0:T(8,128)(2,1)} %w_out_ref.1, f32[32,2048]{1,0:T(8,128)} %get-tuple-element.34.cos_ref, ...), custom_call_target="tpu_custom_call" | custom-call | flops 8053063680 | bytes 23592960 | tf_op jit(solution)/shard_map/back/pallas_call | solution.py:905
  244.5 9.4 %emit.1 = (f32[768,2,768]{2,1,0:T(2,128)}, f32[768,768]{1,0:T(8,128)}, f32[576,768]{1,0:T(8,128)}, f32[192,768]{1,0:T(8,128)}, bf16[512,768]{1,0:T(8,128)(2,1)}, /*index=5*/bf16[512,768]{1,0:T(8,128)(2,1)}) custom-call(bf16[2,3,384,768]{3,2,1,0:T(8,128)(2,1)} %bitcast.11, bf16[2,384,768]{2,1,0:T(8,128)(2,1)} %get-tuple-element.46.small_ref, ...), custom_call_target="tpu_custom_call" | custom-call | bytes 14155776 | tf_op jit(solution)/shard_map/emit/pallas_call | solution.py:998
  253.8 1.5 fusion
  (1 shorter events, 0.0 us)
Async XLA Ops:
  0.6 144.6 %collective-permute-start = (bf16[576,768]{1,0:T(8,128)(2,1)}, bf16[576,768]{1,0:T(8,128)(2,1)S(1)}, u32[]{:S(2)}, u32[]{:S(2)}) collective-permute-start(bf16[576,768]{1,0:T(8,128)(2,1)} %bitcast.17), channel_id=1, source_target_pairs={{0,1},{1,0},{2,3},{3,2},{4,5},{5,4},{6,7},{7,6},{8,9},{9,8},{10,11... | collective-permute-start | bytes 2654216 | tf_op jit(solution)/shard_map/ppermute | solution.py:1039
  145.3 0.9 copy-start

commit v4 on v3

--- a/solution.py
+++ b/solution.py
@@ -204,10 +204,10 @@
 
 
 def first_kernel(
-    size, lengths, tok_ref, cot_ref, ln_ref, w_ref, wo_ref, win_hbm, wdn_hbm,
+    size, lengths, tok_ref, cot_ref, w_ref, wo_ref, win_hbm, wdn_hbm, scale_one_hbm, shift_one_hbm, scale_two_hbm, shift_two_hbm,
     out_ref, dh_ref, slots_ref, norms_ref, total_hbm, x_hbm, q_hbm, k_hbm, v_hbm, q_rows_hbm, att_hbm, cos_hbm, sin_hbm,
     x_ref, win, wdn, wo_near_ref, att, near, outbox, inbox, low, hat, res, own, r1, dlow, give, take, sums,
-    ring_give, ring_take, ring_sems, sems, loads, stores,
+    ring_give, ring_take, ln_ref, ring_sems, sems, loads, stores,
 ):
     rows, width = tok_ref.shape
     hidden = wdn.shape[0] // 2
@@ -240,11 +240,16 @@
         post(W_DOWN, 0, wdn_hbm, wdn.at[pl.ds(hidden, hidden)], core),
     ]
     fetches = []
-    for n, (source, target) in enumerate([(wdn_hbm, wdn.at[pl.ds(0, hidden)])]):
+    moves = [(wdn_hbm, wdn.at[pl.ds(0, hidden)])]
+    for n, source in enumerate((scale_one_hbm, shift_one_hbm, scale_two_hbm, shift_two_hbm)):
+        moves.append((source, ln_ref.at[n]))
+    for n, (source, target) in enumerate(moves):
         fetches.append(pltpu.make_async_copy(source, target, loads.at[n]))
         fetches[-1].start()
     x_ref[0] = tok_ref[...]
     sums[...] = jnp.zeros_like(sums)
+    for fetch in fetches[1:]:
+        fetch.wait()
     scale_one, shift_one, scale_two, shift_two = (ln_ref[i : i + 1, :] for i in range(4))
 
     def branch(slot, other, where):
@@ -277,7 +282,7 @@
         low[0, where, :] = h.astype(BF16)
 
     def attention(raw, q_ref, k_ref, v_ref, k_rows_ref, q_rows_ref, cos_ref, sin_ref, top_ref, acc_ref):
-        fetch = pltpu.make_async_copy(win_hbm, raw, loads.at[1])
+        fetch = pltpu.make_async_copy(win_hbm, raw, loads.at[5])
         fetch.start()
         half_head = HEAD_DIM // 2
         starts, ends, end = [], [], 0
@@ -442,7 +447,7 @@
         pltpu.VMEM((2 * shards, heads, 8, chunk), F32), pltpu.VMEM((2 * shards, heads, 80, chunk), F32),
     )
     normed_copies = [link(NORMED, c, low.at[0, where], low.at[1, where], far) for c, where in enumerate(chunks)]
-    for copy in fetches + weight_copies[1:] + [link(W_IN, 0, win.at[0], win.at[1], core)]:
+    for copy in fetches[:1] + weight_copies[1:] + [link(W_IN, 0, win.at[0], win.at[1], core)]:
         copy.wait()
 
     def feed_forward(gu, hid, total):
@@ -621,7 +626,7 @@
             table,
             table,
         ),
-        in_specs=[pl.BlockSpec(memory_space=pltpu.SMEM)] + [vmem] * 5 + [hbm] * 2,
+        in_specs=[pl.BlockSpec(memory_space=pltpu.SMEM)] + [vmem] * 4 + [hbm] * 6,
         out_specs=[vmem] * 4 + [hbm] * 9,
         scratch_shapes=[
             wide(BF16, shards),
@@ -641,9 +646,11 @@
             pltpu.VMEM((2, chain, width), BF16),
             pltpu.VMEM((2, chain, width), BF16),
             pltpu.VMEM((4, 8, width), F32),
-            *ring_scratch(size, chain, width, RING_EARLY),
+            *ring_scratch(size, chain, width, RING_EARLY)[:2],
+            pltpu.VMEM((8, width), F32),
+            *ring_scratch(size, chain, width, RING_EARLY)[2:],
             dma((2, KINDS, 2)),
-            dma((2,)),
+            dma((6,)),
             dma((8,)),
         ],
         compiler_params=pltpu.CompilerParams(
@@ -653,7 +660,7 @@
             flops=36 * rows * width * hidden, bytes_accessed=40 * rows * width, transcendentals=0
         ),
         name="first",
-    )(lengths, tokens, cotangent, norms, w_turned, w_out, w_in, w_down)
+    )(lengths, tokens, cotangent, w_turned, w_out, w_in, w_down, *norms)
 
 
 class Sum:
@@ -1037,7 +1044,7 @@
     m = lax.axis_index("mp")
     qkv_turned = w_qkv.transpose(1, 2, 0).reshape(3 * local_cols, width)
     qkv_near = lax.ppermute(qkv_turned, "mp", [(i, i ^ 1) for i in range(shards)])
-    norms = jnp.concatenate([jnp.stack([ln1_scale, ln1_shift, ln2_scale, ln2_shift]), jnp.zeros((4, width), F32)])
+    norms = (ln1_scale, ln1_shift, ln2_scale, ln2_shift)
     output, dh, dh_slots, norms, totals, x_slots, q, k, v, q_rows, att, cosine, sine = first(
         lengths, tokens, cotangent, norms, qkv_turned, w_out, w_gate_up, w_down
     )

time: 256 us -> 252 us (0.984)
  local copies, waits for them, and re-layouts: 5.82 us -> 2.43 us
    another operation x4 -> x0, local copies, waits for them, and re-layouts: 2.76 us -> none  [body(): jnp.stack([ln1_scale, ln1_shift, ln2_scale, ln2_shift])]
  transfers between devices with their start and end apart: 1 -> 1, of which waited for: 0 -> 0; matrix products, arithmetic and copies ran while one was open for 1% -> 0% of each run, Pallas kernels for 55% -> 56%
where the time goes in v4:
time: 252 us
  Pallas kernels  248 us (98%)
    pallas_call x1, Pallas kernels, first(): pl.pallas_call(functools.partial(first_kernel, size), out_shape=(shape((r...  141 us
    pallas_call x1, Pallas kernels, back(): pl.pallas_call(functools.partial(back_kernel, size), out_shape=(jax.Shape...  98.2 us
    pallas_call x1, Pallas kernels, emit(): pl.pallas_call(emit_kernel, out_shape=(shape(width, 2, width), shape(widt...  9.38 us
  transfers between devices with their start and end apart: 1, of which 0 were waited for; matrix products, arithmetic and copies ran while one was open for 0% of the time, Pallas kernels for 56%

profile of v4, /device:TPU:0, one launch (start us, length us, event | category | flops | bytes accessed | tf_op | source)
XLA Modules:
  0.0 251.9 jit_solution(2984078411040860160)
XLA Ops:
  0.6 0.5 collective-permute-start
  1.2 140.7 %first.1 = (bf16[512,768]{1,0:T(8,128)(2,1)}, f32[512,768]{1,0:T(8,128)}, bf16[4,512,768]{2,1,0:T(8,128)(2,1)}, f32[8,768]{1,0:T(8,128)}, f32[2,1152,768]{2,1,0:...) custom-call(s32[1,16]{1,0:T(1,128)} %lengths.1, ...), custom_call_target="tpu_custom_call" | custom-call | flops 10871635968 | bytes 15728640 | tf_op jit(solution)/shard_map/first/pallas_call | solution.py:612
  141.9 0.0 collective-permute-done.w_near_ref
  141.9 0.0 copy-start
  141.9 0.9 copy-done
  142.8 98.2 %back.1 = (bf16[512,768]{1,0:T(8,128)(2,1)}, bf16[2,384,768]{2,1,0:T(8,128)(2,1)}, bf16[2,1152,768]{2,1,0:T(8,128)(2,1)}, f32[8,768]{1,0:T(8,128)}) custom-call(bf16[4,192,512]{2,1,0:T(8,128)(2,1)} %get-tuple-element.33.att_ref, bf16[192,768]{1,0:T(8,128)(2,1)} %w_out_ref.1, f32[32,2048]{1,0:T(8,128)} %get-tuple-element.34.cos_ref, ...), custom_call_target="tpu_custom_call" | custom-call | flops 8053063680 | bytes 23592960 | tf_op jit(solution)/shard_map/back/pallas_call | solution.py:912
  241.0 9.4 %emit.1 = (f32[768,2,768]{2,1,0:T(2,128)}, f32[768,768]{1,0:T(8,128)}, f32[576,768]{1,0:T(8,128)}, f32[192,768]{1,0:T(8,128)}, bf16[512,768]{1,0:T(8,128)(2,1)}, /*index=5*/bf16[512,768]{1,0:T(8,128)(2,1)}) custom-call(bf16[2,3,384,768]{3,2,1,0:T(8,128)(2,1)} %bitcast.11, bf16[2,384,768]{2,1,0:T(8,128)(2,1)} %get-tuple-element.46.small_ref, ...), custom_call_target="tpu_custom_call" | custom-call | bytes 14155776 | tf_op jit(solution)/shard_map/emit/pallas_call | solution.py:1005
  250.4 1.5 fusion
Async XLA Ops:
  0.6 141.2 %collective-permute-start = (bf16[576,768]{1,0:T(8,128)(2,1)}, bf16[576,768]{1,0:T(8,128)(2,1)S(1)}, u32[]{:S(2)}, u32[]{:S(2)}) collective-permute-start(bf16[576,768]{1,0:T(8,128)(2,1)} %bitcast.17), channel_id=1, source_target_pairs={{0,1},{1,0},{2,3},{3,2},{4,5},{5,4},{6,7},{7,6},{8,9},{9,8},{10,11... | collective-permute-start | bytes 2654216 | tf_op jit(solution)/shard_map/ppermute | solution.py:1046
  141.9 0.9 copy-start

commit v5 on v4

--- a/solution.py
+++ b/solution.py
@@ -995,7 +995,7 @@
 
 def emit(big, small, output, d_tokens):
     _, chain, width = small.shape
-    steps = 8
+    steps = 4
     per, rows = steps // 2, width // steps
     qkv_steps = steps * 3 // 4
     tokens = output.shape[0] // steps

time: 252 us -> 251 us (level)
  no operation moved by 1% of the time
where the time goes in v5:
time: 251 us; the launch traced here: 250 us
  Pallas kernels  247 us (98%)
    pallas_call x1, Pallas kernels, first(): pl.pallas_call(functools.partial(first_kernel, size), out_shape=(shape((r...  141 us
    pallas_call x1, Pallas kernels, back(): pl.pallas_call(functools.partial(back_kernel, size), out_shape=(jax.Shape...  98.2 us
    pallas_call x1, Pallas kernels, emit(): pl.pallas_call(emit_kernel, out_shape=(shape(width, 2, width), shape(widt...  7.93 us
  transfers between devices with their start and end apart: 1, of which 0 were waited for; matrix products, arithmetic and copies ran while one was open for 0% of the time, Pallas kernels for 56%

profile of v5, /device:TPU:0, one launch (start us, length us, event | category | flops | bytes accessed | tf_op | source)
XLA Modules:
  0.0 250.5 jit_solution(11803496560505829523)
XLA Ops:
  0.6 0.5 collective-permute-start
  1.2 140.7 %first.1 = (bf16[512,768]{1,0:T(8,128)(2,1)}, f32[512,768]{1,0:T(8,128)}, bf16[4,512,768]{2,1,0:T(8,128)(2,1)}, f32[8,768]{1,0:T(8,128)}, f32[2,1152,768]{2,1,0:...) custom-call(s32[1,16]{1,0:T(1,128)} %lengths.1, ...), custom_call_target="tpu_custom_call" | custom-call | flops 10871635968 | bytes 15728640 | tf_op jit(solution)/shard_map/first/pallas_call | solution.py:612
  141.9 0.0 collective-permute-done.w_near_ref
  141.9 0.0 copy-start
  141.9 0.9 copy-done
  142.8 98.2 %back.1 = (bf16[512,768]{1,0:T(8,128)(2,1)}, bf16[2,384,768]{2,1,0:T(8,128)(2,1)}, bf16[2,1152,768]{2,1,0:T(8,128)(2,1)}, f32[8,768]{1,0:T(8,128)}) custom-call(bf16[4,192,512]{2,1,0:T(8,128)(2,1)} %get-tuple-element.33.att_ref, bf16[192,768]{1,0:T(8,128)(2,1)} %w_out_ref.1, f32[32,2048]{1,0:T(8,128)} %get-tuple-element.34.cos_ref, ...), custom_call_target="tpu_custom_call" | custom-call | flops 8053063680 | bytes 23592960 | tf_op jit(solution)/shard_map/back/pallas_call | solution.py:912
  241.0 7.9 %emit.1 = (f32[768,2,768]{2,1,0:T(2,128)}, f32[768,768]{1,0:T(8,128)}, f32[576,768]{1,0:T(8,128)}, f32[192,768]{1,0:T(8,128)}, bf16[512,768]{1,0:T(8,128)(2,1)}, /*index=5*/bf16[512,768]{1,0:T(8,128)(2,1)}) custom-call(bf16[2,3,384,768]{3,2,1,0:T(8,128)(2,1)} %bitcast.11, bf16[2,384,768]{2,1,0:T(8,128)(2,1)} %get-tuple-element.46.small_ref, ...), custom_call_target="tpu_custom_call" | custom-call | bytes 14155776 | tf_op jit(solution)/shard_map/emit/pallas_call | solution.py:1005
  248.9 1.5 fusion
Async XLA Ops:
  0.6 141.2 %collective-permute-start = (bf16[576,768]{1,0:T(8,128)(2,1)}, bf16[576,768]{1,0:T(8,128)(2,1)S(1)}, u32[]{:S(2)}, u32[]{:S(2)}) collective-permute-start(bf16[576,768]{1,0:T(8,128)(2,1)} %bitcast.17), channel_id=1, source_target_pairs={{0,1},{1,0},{2,3},{3,2},{4,5},{5,4},{6,7},{7,6},{8,9},{9,8},{10,11... | collective-permute-start | bytes 2654216 | tf_op jit(solution)/shard_map/ppermute | solution.py:1046
  141.9 0.9 copy-start
